TPU v7x, 32 devices: a whole 2x2x4 slice. The times are simulated.
32 devices in a mesh: dp: 16 (over z, y, x), mp: 2 (over core).
Axes of the slice: x: 2, y: 2, z: 4, core: 2. Of those that a mesh axis runs over, the one named last changes fastest.
Arguments:
- x_input: bfloat16 [32768, 768], P(('dp', 'mp')), may hold values from -6 to 6
- gain_attn: float32 [768], replicated, may hold values from 0.1 to 1.9
- offset_attn: float32 [768], replicated, may hold values from -1.8 to 1.8
- w_qkv: bfloat16 [3, 768, 768], P(None, None, 'mp'), may hold values from -0.21875 to 0.21875
- bias_qv: float32 [2, 768], P(None, 'mp'), may hold values from -1.8 to 1.8
- band_table: float32 [12, 16, 16], P('mp'), may hold values from -4 to 4
- w_proj: bfloat16 [768, 768], P('mp'), may hold values from -0.875 to 0.875
- bias_proj: float32 [768], replicated, may hold values from -1.8 to 1.8
- scale_attn: float32 [768], replicated, may hold values from 0.5 to 1.5
- gain_mlp: float32 [768], replicated, may hold values from 0.1 to 1.9
- offset_mlp: float32 [768], replicated, may hold values from -1.8 to 1.8
- w_up: bfloat16 [768, 3072], P(None, 'mp'), may hold values from -0.21875 to 0.21875
- bias_up: float32 [3072], P('mp'), may hold values from -1.8 to 1.8
- w_down: bfloat16 [3072, 768], P('mp'), may hold values from -0.109375 to 0.109375
- bias_down: float32 [768], replicated, may hold values from -1.8 to 1.8
- scale_mlp: float32 [768], replicated, may hold values from 0.5 to 1.5
- segments: int32 [16, 2048], P('dp'), may hold values from 0 to 11, never falling along the last dimension, each value on 1 to 1024 neighbouring positions
- bands: int32 [16, 2048], P('dp'), may hold values from 0 to 15
- d_output: bfloat16 [32768, 768], P(('dp', 'mp')), may hold values from -6 to 6
Outputs:
- output: bfloat16 [32768, 768], P(('dp', 'mp'))
- grad_input: float32 [32768, 768], P(('dp', 'mp'))
- grad_gain_attn: float32 [768], replicated
- grad_offset_attn: float32 [768], replicated
- grad_w_qkv: float32 [3, 768, 768], P(None, None, 'mp')
- grad_bias_qv: float32 [2, 768], P(None, 'mp')
- grad_band_table: float32 [12, 16, 16], P('mp')
- grad_w_proj: float32 [768, 768], P('mp')
- grad_bias_proj: float32 [768], replicated
- grad_scale_attn: float32 [768], replicated
- grad_gain_mlp: float32 [768], replicated
- grad_offset_mlp: float32 [768], replicated
- grad_w_up: float32 [768, 3072], P(None, 'mp')
- grad_bias_up: float32 [3072], P('mp')
- grad_w_down: float32 [3072, 768], P('mp')
- grad_bias_down: float32 [768], replicated
- grad_scale_mlp: float32 [768], replicated
Inputs may be any that keep to these rules, and one draw needn't show every extreme that they name: `segments`: in each row the ids never fall, each of the 12 ids holds 1 to 1024 patches and one holds exactly 1024; id 12 - 1 marks padding.
All inputs are finite; a program needn't handle non-finite values.
Results may differ from a plain program's by a relative error of at most 0.017.
Values may be sent and summed in bfloat16 or wider, within the bound.
A program may use at most 256 MiB of HBM per device.

v0:
```python
import math

import jax
import jax.numpy as jnp
from jax import lax
from jax.sharding import PartitionSpec as P

PAGES = 12
QBLOCK = 512


norm_eps = 1e-06
masked_score = -1000000000.0


def gelu_tanh(values):
    return (
        0.5
        * values
        * (1.0 + jnp.tanh(0.7978845608028654 * (values + 0.044715 * values * values * values)))
    )


def norm_forward(values, norm_gain, norm_offset):
    center = values - jnp.mean(values, axis=-1, keepdims=True)
    inv_std = lax.rsqrt(jnp.mean(center * center, axis=-1, keepdims=True) + norm_eps)
    scaled = center * inv_std
    return (scaled * norm_gain + norm_offset, scaled, inv_std)


def norm_backward(d_normed, scaled, inv_std, norm_gain):
    d_scaled = d_normed * norm_gain
    mean_grad = jnp.mean(d_scaled, axis=-1, keepdims=True)
    mean_cross = jnp.mean(d_scaled * scaled, axis=-1, keepdims=True)
    d_values = inv_std * (d_scaled - mean_grad - scaled * mean_cross)
    return (d_values, jnp.sum(d_normed * scaled, axis=0), jnp.sum(d_normed, axis=0))


def one_hot(labels, count):
    levels = jnp.arange(count, dtype=jnp.int32)
    return (labels[:, None] == levels[None, :]).astype(jnp.float32)


def split_low(values):
    upper = values.astype(jnp.bfloat16)
    lower = (values - upper.astype(jnp.float32)).astype(jnp.bfloat16)
    return (upper, lower)


def block_scores(
    query_block, segment_block, band_block, keys_row, segment_row, onehot_keys, band_table
):
    factor = 1.0 / math.sqrt(query_block.shape[-1])
    raw_scores = (
        jnp.einsum("qhd,khd->hqk", query_block, keys_row, preferred_element_type=jnp.float32)
        * factor
    )
    onehot_block = one_hot(band_block, band_table.shape[1])
    partial_rows = jnp.sum(onehot_block[None, :, :, None] * band_table[:, None, :, :], axis=2)
    rows_upper, rows_lower = split_low(partial_rows)
    band_bias = jnp.einsum(
        "hqb,kb->hqk", rows_upper, onehot_keys, preferred_element_type=jnp.float32
    ) + jnp.einsum("hqb,kb->hqk", rows_lower, onehot_keys, preferred_element_type=jnp.float32)
    allowed = (segment_block[:, None] == segment_row[None, :]) & (segment_row[None, :] != PAGES - 1)
    return (jnp.where(allowed[None], raw_scores + band_bias, masked_score), onehot_block)


def attend_rows(queries, keys, values, segments, bands, band_table):
    length = segments.shape[1]
    blocks = length // QBLOCK
    heads_here, head_size = (queries.shape[2], queries.shape[3])

    def one_row(inputs):
        query_row, keys_row, values_row, segment_row, band_row = inputs
        onehot_keys = one_hot(band_row, band_table.shape[1]).astype(jnp.bfloat16)

        def one_block(block_inputs):
            query_block, segment_block, band_block = block_inputs
            scores, onehot_block = block_scores(
                query_block,
                segment_block,
                band_block,
                keys_row,
                segment_row,
                onehot_keys,
                band_table,
            )
            row_max = jnp.max(scores, axis=-1, keepdims=True)
            weights = jnp.exp(scores - row_max)
            row_sum = jnp.sum(weights, axis=-1, keepdims=True)
            probability = (weights / row_sum).astype(jnp.bfloat16)
            block_out = jnp.einsum(
                "hqk,khd->qhd", probability, values_row, preferred_element_type=jnp.float32
            )
            return (block_out, (row_max + jnp.log(row_sum))[:, :, 0])

        block_outs, log_norms = lax.map(
            one_block,
            (
                query_row.reshape(blocks, QBLOCK, heads_here, head_size),
                segment_row.reshape(blocks, QBLOCK),
                band_row.reshape(blocks, QBLOCK),
            ),
        )
        return (block_outs.reshape(length, heads_here * head_size), log_norms)

    return lax.map(one_row, (queries, keys, values, segments, bands))


def attend_back(queries, keys, values, segments, bands, band_table, d_attended, log_norms):
    length = segments.shape[1]
    blocks = length // QBLOCK
    heads_here, head_size = (queries.shape[2], queries.shape[3])
    factor = 1.0 / math.sqrt(head_size)

    def one_row(table_acc, inputs):
        query_row, keys_row, values_row, segment_row, band_row, grad_row, norm_row = inputs
        onehot_keys = one_hot(band_row, band_table.shape[1]).astype(jnp.bfloat16)

        def one_block(carry_triple, block_inputs):
            key_acc, value_acc, table_sum = carry_triple
            query_block, segment_block, band_block, grad_block, norm_block = block_inputs
            scores, onehot_block = block_scores(
                query_block,
                segment_block,
                band_block,
                keys_row,
                segment_row,
                onehot_keys,
                band_table,
            )
            probability = jnp.exp(scores - norm_block[:, :, None])
            d_prob = jnp.einsum(
                "qhd,khd->hqk", grad_block, values_row, preferred_element_type=jnp.float32
            )
            delta = jnp.sum(probability * d_prob, axis=-1, keepdims=True)
            d_score = probability * (d_prob - delta)
            d_low, d_rest = split_low(d_score)
            by_key = jnp.einsum(
                "hqk,kb->hqb", d_low, onehot_keys, preferred_element_type=jnp.float32
            ) + jnp.einsum("hqk,kb->hqb", d_rest, onehot_keys, preferred_element_type=jnp.float32)
            table_sum = table_sum + jnp.sum(
                onehot_block[None, :, :, None] * by_key[:, :, None, :], axis=1
            )
            d_query = (
                jnp.einsum("hqk,khd->qhd", d_low, keys_row, preferred_element_type=jnp.float32)
                * factor
            )
            key_acc = (
                key_acc
                + jnp.einsum("hqk,qhd->khd", d_low, query_block, preferred_element_type=jnp.float32)
                * factor
            )
            value_acc = value_acc + jnp.einsum(
                "hqk,qhd->khd",
                probability.astype(jnp.bfloat16),
                grad_block,
                preferred_element_type=jnp.float32,
            )
            return ((key_acc, value_acc, table_sum), d_query)

        zeros_row = jnp.zeros(keys_row.shape, jnp.float32)
        (key_grad, value_grad, table_acc), query_grad = lax.scan(
            one_block,
            (zeros_row, zeros_row, table_acc),
            (
                query_row.reshape(blocks, QBLOCK, heads_here, head_size),
                segment_row.reshape(blocks, QBLOCK),
                band_row.reshape(blocks, QBLOCK),
                grad_row.reshape(blocks, QBLOCK, heads_here, head_size),
                norm_row,
            ),
        )
        return (
            table_acc,
            (
                query_grad.reshape(length, heads_here * head_size),
                key_grad.reshape(length, heads_here * head_size),
                value_grad.reshape(length, heads_here * head_size),
            ),
        )

    return lax.scan(
        one_row,
        jnp.zeros(band_table.shape, jnp.float32),
        (queries, keys, values, segments, bands, d_attended, log_norms),
    )


def body(
    x_input,
    gain_attn,
    offset_attn,
    w_qkv,
    bias_qv,
    band_table,
    w_proj,
    bias_proj,
    scale_attn,
    gain_mlp,
    offset_mlp,
    w_up,
    bias_up,
    w_down,
    bias_down,
    scale_mlp,
    segments,
    bands,
    d_output,
):
    local_rows = x_input.shape[0]
    rows_here, length = segments.shape
    gathered_rows = rows_here * length
    heads_here = band_table.shape[0]
    head_size = w_qkv.shape[2] // heads_here
    head_shape = (rows_here, length, heads_here, head_size)
    position = lax.axis_index("mp") * local_rows
    valid_all = (segments.reshape(gathered_rows) != PAGES - 1).astype(jnp.float32)[:, None]
    valid_local = lax.dynamic_slice_in_dim(valid_all, position, local_rows, 0)
    x_float = x_input.astype(jnp.float32)
    normed_attn, scaled_attn, inv_attn = norm_forward(x_float, gain_attn, offset_attn)
    normed_all = lax.all_gather(normed_attn.astype(jnp.bfloat16), "mp", axis=0, tiled=True)
    projected = jnp.einsum("td,cde->cte", normed_all, w_qkv, preferred_element_type=jnp.float32)
    queries = (projected[0] + bias_qv[0]).astype(jnp.bfloat16).reshape(head_shape)
    keys = projected[1].astype(jnp.bfloat16).reshape(head_shape)
    values = (projected[2] + bias_qv[1]).astype(jnp.bfloat16).reshape(head_shape)
    attended_raw, log_norms = attend_rows(queries, keys, values, segments, bands, band_table)
    attended = (attended_raw.reshape(gathered_rows, -1) * valid_all).astype(jnp.bfloat16)
    attn_out = (
        lax.psum_scatter(
            jnp.dot(attended, w_proj, preferred_element_type=jnp.float32),
            "mp",
            scatter_dimension=0,
            tiled=True,
        )
        + bias_proj
    )
    hidden = x_float + scale_attn * attn_out
    normed_mlp, scaled_mlp, inv_mlp = norm_forward(hidden, gain_mlp, offset_mlp)
    normed_two = lax.all_gather(normed_mlp.astype(jnp.bfloat16), "mp", axis=0, tiled=True)
    pre_act = jnp.dot(normed_two, w_up, preferred_element_type=jnp.float32) + bias_up
    activated_full, gelu_pull = jax.vjp(gelu_tanh, pre_act)
    activated = activated_full.astype(jnp.bfloat16)
    mlp_out = (
        lax.psum_scatter(
            jnp.dot(activated, w_down, preferred_element_type=jnp.float32).astype(jnp.bfloat16),
            "mp",
            scatter_dimension=0,
            tiled=True,
        ).astype(jnp.float32)
        + bias_down
    )
    output = ((hidden + scale_mlp * mlp_out) * valid_local).astype(jnp.bfloat16)
    d_final = d_output.astype(jnp.float32) * valid_local
    grad_scale_mlp = jnp.sum(d_final * mlp_out, axis=0)
    d_mlp = d_final * scale_mlp
    grad_bias_down = jnp.sum(d_mlp, axis=0)
    d_mlp_all = lax.all_gather(d_mlp.astype(jnp.bfloat16), "mp", axis=0, tiled=True)
    grad_w_down = jnp.einsum("tf,td->fd", activated, d_mlp_all, preferred_element_type=jnp.float32)
    d_act = jnp.einsum("td,fd->tf", d_mlp_all, w_down, preferred_element_type=jnp.float32)
    d_pre = gelu_pull(d_act)[0]
    grad_bias_up = jnp.sum(d_pre, axis=0)
    d_pre_low = d_pre.astype(jnp.bfloat16)
    grad_w_up = jnp.einsum("td,tf->df", normed_two, d_pre_low, preferred_element_type=jnp.float32)
    d_normed_mlp = lax.psum_scatter(
        jnp.einsum("tf,df->td", d_pre_low, w_up, preferred_element_type=jnp.float32).astype(
            jnp.bfloat16
        ),
        "mp",
        scatter_dimension=0,
        tiled=True,
    ).astype(jnp.float32)
    d_from_mlp, grad_gain_mlp, grad_offset_mlp = norm_backward(
        d_normed_mlp, scaled_mlp, inv_mlp, gain_mlp
    )
    d_hidden = d_final + d_from_mlp
    grad_scale_attn = jnp.sum(d_hidden * attn_out, axis=0)
    d_attn = d_hidden * scale_attn
    grad_bias_proj = jnp.sum(d_attn, axis=0)
    d_attn_all = lax.all_gather(d_attn.astype(jnp.bfloat16), "mp", axis=0, tiled=True)
    grad_w_proj = jnp.einsum("te,td->ed", attended, d_attn_all, preferred_element_type=jnp.float32)
    d_attended = (
        jnp.einsum("td,ed->te", d_attn_all, w_proj, preferred_element_type=jnp.float32) * valid_all
    ).astype(jnp.bfloat16)
    table_grad, (d_query, d_key, d_value) = attend_back(
        queries,
        keys,
        values,
        segments,
        bands,
        band_table,
        d_attended.reshape(head_shape),
        log_norms,
    )
    d_query = d_query.reshape(gathered_rows, -1)
    d_key = d_key.reshape(gathered_rows, -1)
    d_value = d_value.reshape(gathered_rows, -1)
    grad_bias_qv = jnp.stack([jnp.sum(d_query, axis=0), jnp.sum(d_value, axis=0)])
    d_qkv_low = jnp.stack([d_query, d_key, d_value]).astype(jnp.bfloat16)
    grad_w_qkv = jnp.einsum(
        "td,cte->cde", normed_all, d_qkv_low, preferred_element_type=jnp.float32
    )
    d_normed_attn = lax.psum_scatter(
        jnp.einsum("cte,cde->td", d_qkv_low, w_qkv, preferred_element_type=jnp.float32).astype(
            jnp.bfloat16
        ),
        "mp",
        scatter_dimension=0,
        tiled=True,
    ).astype(jnp.float32)
    d_from_attn, grad_gain_attn, grad_offset_attn = norm_backward(
        d_normed_attn, scaled_attn, inv_attn, gain_attn
    )
    grad_input = d_hidden + d_from_attn
    shared = jnp.stack(
        [
            grad_gain_attn,
            grad_offset_attn,
            grad_bias_proj,
            grad_scale_attn,
            grad_gain_mlp,
            grad_offset_mlp,
            grad_bias_down,
            grad_scale_mlp,
        ]
    )
    summed = lax.psum(
        (
            grad_w_up,
            grad_bias_up,
            grad_w_down,
            grad_w_qkv,
            grad_bias_qv,
            table_grad,
            grad_w_proj,
            shared,
        ),
        "dp",
    )
    shared_sum = lax.psum(summed[7], "mp")
    return (
        output,
        grad_input,
        shared_sum[0],
        shared_sum[1],
        summed[3],
        summed[4],
        summed[5],
        summed[6],
        shared_sum[2],
        shared_sum[3],
        shared_sum[4],
        shared_sum[5],
        summed[0],
        summed[1],
        summed[2],
        shared_sum[6],
        shared_sum[7],
    )


def solution(mesh):
    return jax.shard_map(
        body,
        mesh=mesh,
        in_specs=(
            P(("dp", "mp"), None),
            P(),
            P(),
            P(None, None, "mp"),
            P(None, "mp"),
            P("mp", None, None),
            P("mp", None),
            P(),
            P(),
            P(),
            P(),
            P(None, "mp"),
            P("mp"),
            P("mp", None),
            P(),
            P(),
            P("dp", None),
            P("dp", None),
            P(("dp", "mp"), None),
        ),
        out_specs=(
            P(("dp", "mp"), None),
            P(("dp", "mp"), None),
            P(),
            P(),
            P(None, None, "mp"),
            P(None, "mp"),
            P("mp", None, None),
            P("mp", None),
            P(),
            P(),
            P(),
            P(),
            P(None, "mp"),
            P("mp"),
            P("mp", None),
            P(),
            P(),
        ),
        check_vma=False,
    )
```

profile of v0, /device:TPU:0, one launch (start us, length us, event | category | flops | bytes accessed | tf_op | source)
XLA Modules:
  0.0 1592.8 jit_solution(16777725427815144682)
XLA Ops:
  50.4 344.7 %while.52 = (s32[]{:T(128)}, f32[4,512,6,64]{1,0,3,2:T(4,128)}, f32[4,6,512]{2,1,0:T(8,128)S(1)}, s32[4,512]{1,0:T(4,128)S(1)}, s32[2048]{0:T(1024)S(1)}, /*inde...) while((s32[]{:T(128)}, f32[4,512,6,64]{1,0,3,2:T(4,128)}, ...), condition=%wide.region_6.7_spmd.clone, body=%wide.region_2.6_spmd.clone.sunk | while | flops 2080259072 | bytes 199133392 | solution.py:97
  72.5 26.2 %fusion.175 = (f32[6,512]{1,0:T(8,128)S(1)}, f32[6,512,2048]{2,1,0:T(8,128)}) fusion(f32[6,512,2048]{2,1,0:T(8,128)} %fusion.173, s32[2048]{0:T(1024)S(1)} %get-tuple-element.719, f32[6,512,16]{1,2,0:T(8,128)S(1)} %multiply_reduce_fusion.12, f32[6,512,2048]{2,1,0:T(8,128)} %fusion.174, pred[512,2048]{1,0:T(8,128)(4,1)S(1)} %compare_and_fusion.4), kind=kOutput, calls=%fused_computation.176.clone.1 | convolution fusion | flops 233075712 | bytes 76763136 | tf_op jit(solution)/shard_map/while/body/eval_jaxpr/while/body/eval_jaxpr/hqb,kb->hqk/dot_general | solution.py:63
  120.5 16.1 %dynamic_update_slice.32 = f32[4,512,6,64]{1,0,3,2:T(4,128)} dynamic-update-slice(f32[4,512,6,64]{1,0,3,2:T(4,128)} %get-tuple-element.697, f32[1,512,6,64]{1,0,3,2:T(1,128)S(1)} %copy.99, s32[]{:T(128)S(6)} %copy.106, s32[]{:T(128)} %constant.109.clone.1..sunk, s32[]{:T(128)} %constant.109.clone.1..sunk, s32[]{:T(128)} %constant.109.clone.1..sunk) | dynamic-update-slice | bytes 1572868 | tf_op jit(solution)/shard_map/while/body/eval_jaxpr/while/body/jit(dynamic_update_index_in_dim)/dynamic_update_slice | solution.py:97
  158.7 26.2 %fusion.175 = (f32[6,512]{1,0:T(8,128)S(1)}, f32[6,512,2048]{2,1,0:T(8,128)}) fusion(f32[6,512,2048]{2,1,0:T(8,128)} %fusion.173, s32[2048]{0:T(1024)S(1)} %get-tuple-element.719, f32[6,512,16]{1,2,0:T(8,128)S(1)} %multiply_reduce_fusion.12, f32[6,512,2048]{2,1,0:T(8,128)} %fusion.174, pred[512,2048]{1,0:T(8,128)(4,1)S(1)} %compare_and_fusion.4), kind=kOutput, calls=%fused_computation.176.clone.1 | convolution fusion | flops 233075712 | bytes 76763136 | tf_op jit(solution)/shard_map/while/body/eval_jaxpr/while/body/eval_jaxpr/hqb,kb->hqk/dot_general | solution.py:63
  206.6 16.1 %dynamic_update_slice.32 = f32[4,512,6,64]{1,0,3,2:T(4,128)} dynamic-update-slice(f32[4,512,6,64]{1,0,3,2:T(4,128)} %get-tuple-element.697, f32[1,512,6,64]{1,0,3,2:T(1,128)S(1)} %copy.99, s32[]{:T(128)S(6)} %copy.106, s32[]{:T(128)} %constant.109.clone.1..sunk, s32[]{:T(128)} %constant.109.clone.1..sunk, s32[]{:T(128)} %constant.109.clone.1..sunk) | dynamic-update-slice | bytes 1572868 | tf_op jit(solution)/shard_map/while/body/eval_jaxpr/while/body/jit(dynamic_update_index_in_dim)/dynamic_update_slice | solution.py:97
  244.8 26.2 %fusion.175 = (f32[6,512]{1,0:T(8,128)S(1)}, f32[6,512,2048]{2,1,0:T(8,128)}) fusion(f32[6,512,2048]{2,1,0:T(8,128)} %fusion.173, s32[2048]{0:T(1024)S(1)} %get-tuple-element.719, f32[6,512,16]{1,2,0:T(8,128)S(1)} %multiply_reduce_fusion.12, f32[6,512,2048]{2,1,0:T(8,128)} %fusion.174, pred[512,2048]{1,0:T(8,128)(4,1)S(1)} %compare_and_fusion.4), kind=kOutput, calls=%fused_computation.176.clone.1 | convolution fusion | flops 233075712 | bytes 76763136 | tf_op jit(solution)/shard_map/while/body/eval_jaxpr/while/body/eval_jaxpr/hqb,kb->hqk/dot_general | solution.py:63
  292.7 16.1 %dynamic_update_slice.32 = f32[4,512,6,64]{1,0,3,2:T(4,128)} dynamic-update-slice(f32[4,512,6,64]{1,0,3,2:T(4,128)} %get-tuple-element.697, f32[1,512,6,64]{1,0,3,2:T(1,128)S(1)} %copy.99, s32[]{:T(128)S(6)} %copy.106, s32[]{:T(128)} %constant.109.clone.1..sunk, s32[]{:T(128)} %constant.109.clone.1..sunk, s32[]{:T(128)} %constant.109.clone.1..sunk) | dynamic-update-slice | bytes 1572868 | tf_op jit(solution)/shard_map/while/body/eval_jaxpr/while/body/jit(dynamic_update_index_in_dim)/dynamic_update_slice | solution.py:97
  330.9 26.3 %fusion.175 = (f32[6,512]{1,0:T(8,128)S(1)}, f32[6,512,2048]{2,1,0:T(8,128)}) fusion(f32[6,512,2048]{2,1,0:T(8,128)} %fusion.173, s32[2048]{0:T(1024)S(1)} %get-tuple-element.719, f32[6,512,16]{1,2,0:T(8,128)S(1)} %multiply_reduce_fusion.12, f32[6,512,2048]{2,1,0:T(8,128)} %fusion.174, pred[512,2048]{1,0:T(8,128)(4,1)S(1)} %compare_and_fusion.4), kind=kOutput, calls=%fused_computation.176.clone.1 | convolution fusion | flops 233075712 | bytes 76763136 | tf_op jit(solution)/shard_map/while/body/eval_jaxpr/while/body/eval_jaxpr/hqb,kb->hqk/dot_general | solution.py:63
  378.9 16.1 %dynamic_update_slice.32 = f32[4,512,6,64]{1,0,3,2:T(4,128)} dynamic-update-slice(f32[4,512,6,64]{1,0,3,2:T(4,128)} %get-tuple-element.697, f32[1,512,6,64]{1,0,3,2:T(1,128)S(1)} %copy.99, s32[]{:T(128)S(6)} %copy.106, s32[]{:T(128)} %constant.109.clone.1..sunk, s32[]{:T(128)} %constant.109.clone.1..sunk, s32[]{:T(128)} %constant.109.clone.1..sunk) | dynamic-update-slice | bytes 1572868 | tf_op jit(solution)/shard_map/while/body/eval_jaxpr/while/body/jit(dynamic_update_index_in_dim)/dynamic_update_slice | solution.py:97
  410.1 15.3 reduce-scatter.5.cloned.1.call-done
  446.1 13.7 multiply_convert_fusion
  461.4 19.4 %fusion.106 = (f32[1536]{0:T(1024)}, bf16[2048,1536]{1,0:T(8,128)(2,1)S(1)}) fusion(bf16[2048,768]{1,0:T(8,128)(2,1)} %all-gather.9.cloned.1.call-done, bf16[1536,768]{1,0:T(8,128)(2,1)} %param.36, f32[2048,1536]{1,0:T(8,128)} %get-tuple-element.502, f32[1536]{0:T(1024)S(1)} %copy-done.50), kind=kOutput, calls=%fused_computation.180 | convolution fusion | flops 4913625600 | bytes 24391680 | tf_op jit(solution)/shard_map/td,fd->tf/dot_general | solution.py:260
  528.2 13.5 all-gather.11.cloned.1.call-done
  554.0 565.8 %while.53 = (s32[]{:T(128)}, f32[2048,6,64]{0,2,1:T(8,128)}, f32[2048,6,64]{0,2,1:T(8,128)}, f32[6,16,16]{2,1,0:T(8,128)S(1)}, f32[4,512,6,64]{1,3,2,0:T(8,128)}...) while((s32[]{:T(128)}, f32[2048,6,64]{0,2,1:T(8,128)}, ...), condition=%wide.region_18.19_spmd.clone, body=%wide.region_14.18_spmd.clone.sunk | while | flops 4942529024 | bytes 438704416 | solution.py:163
  555.8 13.3 fusion.193
  590.9 34.7 %multiply_reduce_fusion.14 = (f32[6,512]{1,0:T(8,128)S(1)}, f32[6,512,2048]{2,1,0:T(8,128)}) fusion(f32[6,512,2048]{2,1,0:T(8,128)} %fusion.193, f32[6,512]{1,0:T(8,128)S(1)} %dynamic-slice_bitcast_fusion.2, f32[6,512,2048]{2,1,0:T(8,128)} %fusion.195, s32[2048]{0:T(1024)} %copy-done.13, f32[6,512,16]{1,2,0:T(8,128)S(1)} %multiply_reduce_fusion.13, ...), kind=kOutput, calls=%fused_computation.31.clone.1 | convolution fusion | flops 245658624 | bytes 101941248 | tf_op jit(solution)/shard_map/while/body/eval_jaxpr/while/body/eval_jaxpr/hqb,kb->hqk/dot_general | solution.py:63
  637.8 16.1 %fusion.197 = bf16[6,512,2048]{2,1,0:T(8,128)(2,1)S(1)} fusion(f32[6,512,2048]{2,1,0:T(8,128)} %get-tuple-element.681, f32[6,512,2048]{2,1,0:T(8,128)} %fusion.193, f32[6,512]{1,0:T(8,128)S(1)} %get-tuple-element.682), kind=kLoop, calls=%fused_computation.36.clone.1 | loop fusion | flops 18874368 | bytes 62926848 | tf_op jit(solution)/shard_map/while/body/eval_jaxpr/while/body/eval_jaxpr/convert_element_type | solution.py:45
  653.9 22.0 %fusion.198 = f32[6,512,16]{1,2,0:T(8,128)S(1)} fusion(bf16[6,512,2048]{2,1,0:T(8,128)(2,1)S(1)} %fusion.197, f32[6,512,2048]{2,1,0:T(8,128)} %get-tuple-element.681, f32[6,512,2048]{2,1,0:T(8,128)} %fusion.193, f32[6,512]{1,0:T(8,128)S(1)} %get-tuple-element.682, s32[2048]{0:T(1024)S(1)} %copy-done.14), kind=kOutput, calls=%fused_computation.33.clone.1 | convolution fusion | flops 232882176 | bytes 63131648 | tf_op jit(solution)/shard_map/while/body/eval_jaxpr/while/body/eval_jaxpr/hqk,kb->hqb/dot_general | solution.py:141
  695.6 13.3 fusion.193
  730.7 34.7 %multiply_reduce_fusion.14 = (f32[6,512]{1,0:T(8,128)S(1)}, f32[6,512,2048]{2,1,0:T(8,128)}) fusion(f32[6,512,2048]{2,1,0:T(8,128)} %fusion.193, f32[6,512]{1,0:T(8,128)S(1)} %dynamic-slice_bitcast_fusion.2, f32[6,512,2048]{2,1,0:T(8,128)} %fusion.195, s32[2048]{0:T(1024)} %copy-done.13, f32[6,512,16]{1,2,0:T(8,128)S(1)} %multiply_reduce_fusion.13, ...), kind=kOutput, calls=%fused_computation.31.clone.1 | convolution fusion | flops 245658624 | bytes 101941248 | tf_op jit(solution)/shard_map/while/body/eval_jaxpr/while/body/eval_jaxpr/hqb,kb->hqk/dot_general | solution.py:63
  778.6 16.1 %fusion.197 = bf16[6,512,2048]{2,1,0:T(8,128)(2,1)S(1)} fusion(f32[6,512,2048]{2,1,0:T(8,128)} %get-tuple-element.681, f32[6,512,2048]{2,1,0:T(8,128)} %fusion.193, f32[6,512]{1,0:T(8,128)S(1)} %get-tuple-element.682), kind=kLoop, calls=%fused_computation.36.clone.1 | loop fusion | flops 18874368 | bytes 62926848 | tf_op jit(solution)/shard_map/while/body/eval_jaxpr/while/body/eval_jaxpr/convert_element_type | solution.py:45
  794.7 22.0 %fusion.198 = f32[6,512,16]{1,2,0:T(8,128)S(1)} fusion(bf16[6,512,2048]{2,1,0:T(8,128)(2,1)S(1)} %fusion.197, f32[6,512,2048]{2,1,0:T(8,128)} %get-tuple-element.681, f32[6,512,2048]{2,1,0:T(8,128)} %fusion.193, f32[6,512]{1,0:T(8,128)S(1)} %get-tuple-element.682, s32[2048]{0:T(1024)S(1)} %copy-done.14), kind=kOutput, calls=%fused_computation.33.clone.1 | convolution fusion | flops 232882176 | bytes 63131648 | tf_op jit(solution)/shard_map/while/body/eval_jaxpr/while/body/eval_jaxpr/hqk,kb->hqb/dot_general | solution.py:141
  837.4 13.3 fusion.193
  872.5 34.7 %multiply_reduce_fusion.14 = (f32[6,512]{1,0:T(8,128)S(1)}, f32[6,512,2048]{2,1,0:T(8,128)}) fusion(f32[6,512,2048]{2,1,0:T(8,128)} %fusion.193, f32[6,512]{1,0:T(8,128)S(1)} %dynamic-slice_bitcast_fusion.2, f32[6,512,2048]{2,1,0:T(8,128)} %fusion.195, s32[2048]{0:T(1024)} %copy-done.13, f32[6,512,16]{1,2,0:T(8,128)S(1)} %multiply_reduce_fusion.13, ...), kind=kOutput, calls=%fused_computation.31.clone.1 | convolution fusion | flops 245658624 | bytes 101941248 | tf_op jit(solution)/shard_map/while/body/eval_jaxpr/while/body/eval_jaxpr/hqb,kb->hqk/dot_general | solution.py:63
  920.3 16.1 %fusion.197 = bf16[6,512,2048]{2,1,0:T(8,128)(2,1)S(1)} fusion(f32[6,512,2048]{2,1,0:T(8,128)} %get-tuple-element.681, f32[6,512,2048]{2,1,0:T(8,128)} %fusion.193, f32[6,512]{1,0:T(8,128)S(1)} %get-tuple-element.682), kind=kLoop, calls=%fused_computation.36.clone.1 | loop fusion | flops 18874368 | bytes 62926848 | tf_op jit(solution)/shard_map/while/body/eval_jaxpr/while/body/eval_jaxpr/convert_element_type | solution.py:45
  936.5 22.0 %fusion.198 = f32[6,512,16]{1,2,0:T(8,128)S(1)} fusion(bf16[6,512,2048]{2,1,0:T(8,128)(2,1)S(1)} %fusion.197, f32[6,512,2048]{2,1,0:T(8,128)} %get-tuple-element.681, f32[6,512,2048]{2,1,0:T(8,128)} %fusion.193, f32[6,512]{1,0:T(8,128)S(1)} %get-tuple-element.682, s32[2048]{0:T(1024)S(1)} %copy-done.14), kind=kOutput, calls=%fused_computation.33.clone.1 | convolution fusion | flops 232882176 | bytes 63131648 | tf_op jit(solution)/shard_map/while/body/eval_jaxpr/while/body/eval_jaxpr/hqk,kb->hqb/dot_general | solution.py:141
  979.2 13.3 fusion.193
  1014.3 34.7 %multiply_reduce_fusion.14 = (f32[6,512]{1,0:T(8,128)S(1)}, f32[6,512,2048]{2,1,0:T(8,128)}) fusion(f32[6,512,2048]{2,1,0:T(8,128)} %fusion.193, f32[6,512]{1,0:T(8,128)S(1)} %dynamic-slice_bitcast_fusion.2, f32[6,512,2048]{2,1,0:T(8,128)} %fusion.195, s32[2048]{0:T(1024)} %copy-done.13, f32[6,512,16]{1,2,0:T(8,128)S(1)} %multiply_reduce_fusion.13, ...), kind=kOutput, calls=%fused_computation.31.clone.1 | convolution fusion | flops 245658624 | bytes 101941248 | tf_op jit(solution)/shard_map/while/body/eval_jaxpr/while/body/eval_jaxpr/hqb,kb->hqk/dot_general | solution.py:63
  1062.1 16.1 %fusion.197 = bf16[6,512,2048]{2,1,0:T(8,128)(2,1)S(1)} fusion(f32[6,512,2048]{2,1,0:T(8,128)} %get-tuple-element.681, f32[6,512,2048]{2,1,0:T(8,128)} %fusion.193, f32[6,512]{1,0:T(8,128)S(1)} %get-tuple-element.682), kind=kLoop, calls=%fused_computation.36.clone.1 | loop fusion | flops 18874368 | bytes 62926848 | tf_op jit(solution)/shard_map/while/body/eval_jaxpr/while/body/eval_jaxpr/convert_element_type | solution.py:45
  1078.2 22.0 %fusion.198 = f32[6,512,16]{1,2,0:T(8,128)S(1)} fusion(bf16[6,512,2048]{2,1,0:T(8,128)(2,1)S(1)} %fusion.197, f32[6,512,2048]{2,1,0:T(8,128)} %get-tuple-element.681, f32[6,512,2048]{2,1,0:T(8,128)} %fusion.193, f32[6,512]{1,0:T(8,128)S(1)} %get-tuple-element.682, s32[2048]{0:T(1024)S(1)} %copy-done.14), kind=kOutput, calls=%fused_computation.33.clone.1 | convolution fusion | flops 232882176 | bytes 63131648 | tf_op jit(solution)/shard_map/while/body/eval_jaxpr/while/body/eval_jaxpr/hqk,kb->hqb/dot_general | solution.py:141
  1179.8 84.4 %all-reduce = (f32[8,768]{1,0:T(8,128)S(1)}, f32[2,384]{1,0:T(2,128)}, f32[6,16,16]{2,1,0:T(8,128)}, f32[1536]{0:T(1024)}) all-reduce(f32[8,768]{1,0:T(8,128)S(1)} %stack.49, f32[2,384]{1,0:T(2,128)S(1)} %pad_maximum_fusion.3, f32[6,16,16]{2,1,0:T(8,128)S(1)} %get-tuple-element.226, ...), channel_id=1, replica_groups=mesh['dp'=16,'mp'=2] {'dp'}, use_global_device_ids=true, to_apply=%region_30.31 | all-reduce | flops 9984 | bytes 79872 | tf_op jit(solution)/shard_map/psum | solution.py:327
  1272.4 299.7 %all-reduce.4.cloned.1.call-done = (f32[3,768,384]{1,2,0:T(8,128)}, f32[384,768]{1,0:T(8,128)}, f32[768,1536]{1,0:T(8,128)}, f32[1536,768]{1,0:T(8,128)}) async-done(((f32[3,768,384]{1,2,0:T(8,128)}, f32[384,768]{1,0:T(8,128)}, f32[768,1536]{1,0:T(8,128)}, f32[1536,768]{1,0:T(8,128)}), (f32[3,768,384]{1,2,0:T(8,128)}, f32[384,768]{1,0:T(8,128)}, f32[768,1536]{1,0:T(8,128)}, ...) | async-done | bytes 14155792 | tf_op jit(solution)/shard_map/psum | solution.py:327
  (344 shorter events, 617.5 us)
Async XLA Ops:
  7.2 438.9 %copy-start = (bf16[768,1536]{1,0:T(8,128)(2,1)S(1)}, bf16[768,1536]{1,0:T(8,128)(2,1)}, u32[]{:S(2)}) copy-start(bf16[768,1536]{1,0:T(8,128)(2,1)} %param.34) | copy-start | bytes 7077892
  7.2 20.8 %all-gather.5.cloned.1.call-start = ((), (), s32[]{:S(2)}) async-start(), calls=%async_computation.4 | async-start | bytes 4718592 | tf_op jit(solution)/shard_map/all_gather | solution.py:222
  11.2 23.3 %copy-start.27 = (f32[1024]{0:T(1024)}, f32[1024]{0:T(1024)S(1)}, u32[]{:S(2)}) copy-start(f32[1024]{0:T(1024)S(1)} %add_rsqrt_fusion.1) | copy-start | bytes 12292
  13.1 412.4 %reduce-scatter.5.cloned.1.call-start = ((), (), s32[]{:S(2)}) async-start(), calls=%async_computation.5 | async-start | bytes 9437184 | tf_op jit(solution)/shard_map/reduce_scatter | solution.py:230
  51.4 10.1 copy-start.3
  98.8 10.5 copy-start.5
  137.6 10.1 copy-start.3
  184.9 10.5 copy-start.5
  223.7 10.1 copy-start.3
  271.0 10.5 copy-start.5
  309.8 10.1 copy-start.3
  357.2 10.5 copy-start.5
  410.1 15.4 copy-start.32
  410.1 15.4 copy-start.35
  410.1 36.0 %all-gather.7.cloned.1.call-start = ((), (), s32[]{:S(2)}) async-start(), calls=%async_computation.6 | async-start | bytes 4718592 | tf_op jit(solution)/shard_map/all_gather | solution.py:240
  431.8 14.3 copy-start.50
  431.8 29.6 %all-gather.9.cloned.1.call-start = ((), (), s32[]{:S(2)}) async-start(), calls=%async_computation.8 | async-start | bytes 4718592 | tf_op jit(solution)/shard_map/all_gather | solution.py:258
  434.9 67.5 %reduce-scatter.9.cloned.1.call-start = ((), (), s32[]{:S(2)}) async-start(), calls=%async_computation.9 | async-start | bytes 4718592 | tf_op jit(solution)/shard_map/reduce_scatter | solution.py:265
  489.9 27.6 %reduce-scatter.7.cloned.1.call-start = ((), (), s32[]{:S(2)}) async-start(), calls=%async_computation.7 | async-start | bytes 4718592 | tf_op jit(solution)/shard_map/reduce_scatter | solution.py:245
  500.8 16.8 %copy-start.15 = (bf16[1024,768]{1,0:T(8,128)(2,1)S(1)}, bf16[1024,768]{1,0:T(8,128)(2,1)}, u32[]{:S(2)}) copy-start(bf16[1024,768]{1,0:T(8,128)(2,1)} %param.41) | copy-start | bytes 4718596
  500.8 16.8 %copy-start.44 = (f32[768]{0:T(1024)S(1)}, f32[768]{0:T(1024)}, u32[]{:S(2)}) copy-start(f32[768]{0:T(1024)} %param.37) | copy-start | bytes 9220
  500.8 40.9 %all-gather.11.cloned.1.call-start = ((), (), s32[]{:S(2)}) async-start(), calls=%async_computation.10 | async-start | bytes 4718592 | tf_op jit(solution)/shard_map/all_gather | solution.py:280
  528.1 648.2 %reduce-scatter.11.cloned.1.call-start = ((), (), s32[]{:S(2)}) async-start(), calls=%async_computation.11 | async-start | bytes 4718592 | tf_op jit(solution)/shard_map/reduce_scatter | solution.py:303
  637.8 16.1 %copy-start.14 = (s32[2048]{0:T(1024)S(1)}, s32[2048]{0:T(1024)}, u32[]{:S(2)}) copy-start(s32[2048]{0:T(1024)} %copy-done.13) | copy-start | bytes 24580 | tf_op jit(solution)/shard_map/while/body/eval_jaxpr/while
  653.9 25.7 %copy-start.2 = (bf16[6,512,2048]{2,1,0:T(8,128)(2,1)}, bf16[6,512,2048]{2,1,0:T(8,128)(2,1)S(1)}, u32[]{:S(2)}) copy-start(bf16[6,512,2048]{2,1,0:T(8,128)(2,1)S(1)} %fusion.197) | copy-start | bytes 37748740 | tf_op jit(solution)/shard_map/while/body/eval_jaxpr/while
  778.6 16.1 %copy-start.14 = (s32[2048]{0:T(1024)S(1)}, s32[2048]{0:T(1024)}, u32[]{:S(2)}) copy-start(s32[2048]{0:T(1024)} %copy-done.13) | copy-start | bytes 24580 | tf_op jit(solution)/shard_map/while/body/eval_jaxpr/while
  794.7 25.7 %copy-start.2 = (bf16[6,512,2048]{2,1,0:T(8,128)(2,1)}, bf16[6,512,2048]{2,1,0:T(8,128)(2,1)S(1)}, u32[]{:S(2)}) copy-start(bf16[6,512,2048]{2,1,0:T(8,128)(2,1)S(1)} %fusion.197) | copy-start | bytes 37748740 | tf_op jit(solution)/shard_map/while/body/eval_jaxpr/while
  920.3 16.1 %copy-start.14 = (s32[2048]{0:T(1024)S(1)}, s32[2048]{0:T(1024)}, u32[]{:S(2)}) copy-start(s32[2048]{0:T(1024)} %copy-done.13) | copy-start | bytes 24580 | tf_op jit(solution)/shard_map/while/body/eval_jaxpr/while
  936.4 25.7 %copy-start.2 = (bf16[6,512,2048]{2,1,0:T(8,128)(2,1)}, bf16[6,512,2048]{2,1,0:T(8,128)(2,1)S(1)}, u32[]{:S(2)}) copy-start(bf16[6,512,2048]{2,1,0:T(8,128)(2,1)S(1)} %fusion.197) | copy-start | bytes 37748740 | tf_op jit(solution)/shard_map/while/body/eval_jaxpr/while
  1062.1 16.1 %copy-start.14 = (s32[2048]{0:T(1024)S(1)}, s32[2048]{0:T(1024)}, u32[]{:S(2)}) copy-start(s32[2048]{0:T(1024)} %copy-done.13) | copy-start | bytes 24580 | tf_op jit(solution)/shard_map/while/body/eval_jaxpr/while
  1078.2 25.7 %copy-start.2 = (bf16[6,512,2048]{2,1,0:T(8,128)(2,1)}, bf16[6,512,2048]{2,1,0:T(8,128)(2,1)S(1)}, u32[]{:S(2)}) copy-start(bf16[6,512,2048]{2,1,0:T(8,128)(2,1)S(1)} %fusion.197) | copy-start | bytes 37748740 | tf_op jit(solution)/shard_map/while/body/eval_jaxpr/while
  1146.6 425.5 %all-reduce.4.cloned.1.call-start = ((), (), s32[]{:S(2)}) async-start(), calls=%async_computation.12 | async-start | bytes 28311552 | tf_op jit(solution)/shard_map/psum | solution.py:327
  (46 other events, 153.4 us)
Sparse Core Ops, SparseCore 0:
  13.2 14.8 all-gather.4
  410.2 15.1 reduce-scatter.4
  431.9 14.1 all-gather.6
  448.1 13.2 all-gather.8
  490.1 12.3 reduce-scatter.8
  505.1 12.4 reduce-scatter.6
  528.2 13.3 all-gather.10
  1146.8 12.3 reduce-scatter.10
  1175.6 396.4 all-reduce.3
where the time goes:
time: 1600 us; the launch traced here: 1590 us
  matrix products  825 us (52%)
  waiting for transfers between devices  366 us (23%)
  other arithmetic  166 us (10%)
  local copies, waits for them, and re-layouts  132 us (8%)
  blocking collectives  87.8 us (5%)
    psum x1, waiting for transfers between devices, body(): lax.psum((grad_w_up, grad_bias_up, grad_w_down, grad_w_qkv, grad_bias_qv,...  300 us
    dot_general x8, matrix products, block_scores(): jnp.einsum('hqb,kb->hqk', rows_lower, onehot_keys, preferred_element_type...  244 us
    dot_general x8, matrix products, block_scores(): jnp.einsum('qhd,khd->hqk', query_block, keys_row, preferred_element_type=...  88.3 us
    dot_general x4, matrix products, one_block(): jnp.einsum('hqk,kb->hqb', d_rest, onehot_keys, preferred_element_type=jnp...  87.9 us
    psum x1, blocking collectives, body(): lax.psum((grad_w_up, grad_bias_up, grad_w_down, grad_w_qkv, grad_bias_qv,...  84.4 us
    dot_general x8, matrix products, block_scores(): jnp.einsum('hqb,kb->hqk', rows_upper, onehot_keys, preferred_element_type...  83.2 us
    dynamic_update_slice x8, local copies, waits for them, and re-layouts, one_row(): lax.map(one_block, (query_row.reshape(blocks, QBLOCK, heads_here, head_si...  67.4 us
    convert_element_type x4, other arithmetic, split_low(): upper = values.astype(jnp.bfloat16)  64.4 us
  transfers between devices with their start and end apart: 9, of which 8 were waited for; matrix products, arithmetic and copies ran while one was open for 4% of the time, Pallas kernels for 0%

commit v1 on v0

v1 whole, which is shorter than its diff:
```python
import functools
import jax
import jax.numpy as jnp
from jax import lax
from jax.sharding import PartitionSpec as P
from jax.experimental import pallas as pl
from jax.experimental.pallas import tpu as pltpu
PAGES = 12
BLK = 256
masked_score = -1000000000.0
f32, bf16, i32 = jnp.float32, jnp.bfloat16, jnp.int32

def nn(a, b):
    return lax.dot_general(a, b, (((1,), (0,)), ((), ())), preferred_element_type=f32)

def nt(a, b):
    return lax.dot_general(a, b, (((1,), (1,)), ((), ())), preferred_element_type=f32)

def block_ranges(segments):
    rows, length = segments.shape
    first = segments[:, ::BLK]
    last = jnp.minimum(segments[:, BLK - 1 :: BLK], PAGES - 2)
    start = jnp.sum((segments[:, None, :] < first[:, :, None]).astype(i32), -1)
    stop = jnp.sum((segments[:, None, :] <= last[:, :, None]).astype(i32), -1)
    lo = start // BLK
    hi = jnp.where(stop > start, (stop + BLK - 1) // BLK, lo)
    return lo, hi

def split3(v):
    a = v.astype(bf16)
    r = v - a.astype(f32)
    b = r.astype(bf16)
    c = (r - b.astype(f32)).astype(bf16)
    return a, b, c

def features(seg, band, nb):
    length = seg.shape[1]
    rows = lax.broadcasted_iota(i32, (16, length), 0)
    one_band = jnp.where(rows == band, 1.0, 0.0).astype(f32)
    one_seg = jnp.where(rows == seg, 1.0, 0.0).astype(f32)
    same = (rows == seg) & (rows != PAGES - 1)
    mask = jnp.where(same | (rows >= PAGES), 0.0, masked_score).astype(f32)
    return one_band, one_seg, mask

def fwd_kernel(lo_ref, hi_ref, q_ref, k_ref, v_ref, seg_ref, band_ref, tab_ref, o_ref, ot_ref, ln_ref,
               kx, qx, vx):
    length = q_ref.shape[0]
    row = pl.program_id(0)
    seg = seg_ref[...]
    band = band_ref[...]
    one_band, one_seg, mask = features(seg, band, 16)
    tail = jnp.where(lax.broadcasted_iota(i32, (16, length), 0) < 3, 1.0, 0.0).astype(f32)
    auxt = jnp.concatenate([one_band, one_band, one_seg, tail], axis=0)
    aux = jnp.concatenate([auxt, auxt], axis=0).T.astype(bf16)
    lane = lax.broadcasted_iota(i32, (length, 128), 1)
    k = k_ref[...]
    left = lane < 64
    kx[0] = jnp.where(left, k, aux)
    kx[1] = jnp.where(left, aux, k)
    qt = q_ref[...].astype(f32).T.astype(bf16)
    vt = v_ref[...].astype(f32).T.astype(bf16)
    oh = one_band.astype(bf16)
    zeros16 = jnp.zeros((16, length), bf16)
    for h in range(2):
        rows = nn(tab_ref[h], oh).astype(bf16)
        base = 64 * h
        qx[h, base : base + 64, :] = qt[base : base + 64]
        other = 64 - base
        qx[h, other : other + 32, :] = rows
        qx[h, other + 32 : other + 48, :] = mask.astype(bf16)
        qx[h, other + 48 : other + 64, :] = zeros16
        vx[h, 0:64, :] = vt[base : base + 64]
        vx[h, 64:80, :] = jnp.ones((16, length), bf16)

    def qblock(qb, _):
        qo = pl.multiple_of(qb * BLK, BLK)
        q0 = qx[0, :, pl.ds(qo, BLK)]
        q1 = qx[1, :, pl.ds(qo, BLK)]
        qs = (q0, q1)

        def kblock(kb, carry):
            ko = pl.multiple_of(kb * BLK, BLK)
            out = []
            for h in range(2):
                m, acc = carry[2 * h], carry[2 * h + 1]
                s = nn(kx[h, pl.ds(ko, BLK), :], qs[h])
                m_new = jnp.maximum(m, jnp.max(s, axis=0, keepdims=True))
                p = jnp.exp(s - m_new).astype(bf16)
                alpha = jnp.exp(m - m_new)
                acc = acc * alpha + nn(vx[h, :, pl.ds(ko, BLK)], p)
                out += [m_new, acc]
            return tuple(out)

        init = (jnp.full((1, BLK), -3e38, f32), jnp.zeros((80, BLK), f32)) * 2
        m0, a0, m1, a1 = lax.fori_loop(lo_ref[row, qb], hi_ref[row, qb], kblock, init)
        valid = seg_ref[:, pl.ds(qo, BLK)] != PAGES - 1
        outs = []
        for h, (m, a) in enumerate(((m0, a0), (m1, a1))):
            total = jnp.where(valid, a[64:65], 1.0)
            outs.append(jnp.where(valid, a[:64] / total, 0.0))
            ln_ref[h : h + 1, pl.ds(qo, BLK)] = jnp.where(valid, m + jnp.log(total), 0.0)
        ot = jnp.concatenate(outs, axis=0)
        ot_ref[:, pl.ds(qo, BLK)] = ot
        o_ref[pl.ds(qo, BLK), :] = ot.T.astype(bf16)
        return 0

    lax.fori_loop(0, length // BLK, qblock, 0)

def attend(qkv, segments, bands, tab):
    _, rows, length, width = qkv.shape
    pairs = width // 128
    lo, hi = block_ranges(segments)
    seg3 = segments.reshape(rows, 1, length)
    band3 = bands.reshape(rows, 1, length)
    part = lambda c: pl.BlockSpec((None, None, length, 128), lambda r, p, *_: (c, r, 0, p))
    rowspec = pl.BlockSpec((None, 1, length), lambda r, p, *_: (r, 0, 0))
    return pl.pallas_call(
        fwd_kernel,
        out_shape=(
            jax.ShapeDtypeStruct((rows, length, width), bf16),
            jax.ShapeDtypeStruct((rows, width, length), f32),
            jax.ShapeDtypeStruct((rows, pairs, 2, length), f32),
        ),
        grid_spec=pltpu.PrefetchScalarGridSpec(
            num_scalar_prefetch=2,
            grid=(rows, pairs),
            in_specs=[part(0), part(1), part(2), rowspec, rowspec,
                      pl.BlockSpec((2, 32, 16), lambda r, p, *_: (p, 0, 0))],
            out_specs=[
                pl.BlockSpec((None, length, 128), lambda r, p, *_: (r, 0, p)),
                pl.BlockSpec((None, 128, length), lambda r, p, *_: (r, p, 0)),
                pl.BlockSpec((None, None, 2, length), lambda r, p, *_: (r, p, 0, 0)),
            ],
            scratch_shapes=[
                pltpu.VMEM((2, length, 128), bf16),
                pltpu.VMEM((2, 128, length), bf16),
                pltpu.VMEM((2, 80, length), bf16),
            ],
        ),
        name="attend",
    )(lo, hi, qkv, qkv, qkv, seg3, band3, tab)

def bwd_kernel(lo_ref, hi_ref, q_ref, k_ref, v_ref, seg_ref, band_ref, tab_ref, do_ref, ot_ref, ln_ref,
               dqkv_ref, bias_ref, table_ref,
               kx, qx, vx, dox, kt, qm, dom, dqt):
    length = q_ref.shape[0]
    row = pl.program_id(0)
    seg = seg_ref[...]
    band = band_ref[...]
    one_band, one_seg, mask = features(seg, band, 16)
    tail = jnp.where(lax.broadcasted_iota(i32, (16, length), 0) < 3, 1.0, 0.0).astype(f32)
    auxt = jnp.concatenate([one_band, one_band, one_seg, tail], axis=0)
    aux = jnp.concatenate([auxt, auxt], axis=0).T.astype(bf16)
    lane = lax.broadcasted_iota(i32, (length, 128), 1)
    left = lane < 64
    k = k_ref[...]
    q = q_ref[...]
    v = v_ref[...]
    do = do_ref[...]
    zero = jnp.zeros_like(k)
    one = jnp.ones_like(k)
    kx[0] = jnp.where(left, k, aux)
    kx[1] = jnp.where(left, aux, k)
    vx[0] = jnp.where(left, v, jnp.where(lane < 67, one, zero))
    vx[1] = jnp.where(left, jnp.where(lane < 3, one, zero), v)
    qm[0] = jnp.where(left, q, zero)
    qm[1] = jnp.where(left, zero, q)
    dom[0] = jnp.where(left, do, zero)
    dom[1] = jnp.where(left, zero, do)
    qt = q.astype(f32).T.astype(bf16)
    ktt = k.astype(f32).T.astype(bf16)
    dot = do.astype(f32).T
    dotl = dot.astype(bf16)
    oh = one_band.astype(bf16)
    prod = dot * ot_ref[...]
    rows16 = lax.broadcasted_iota(i32, (16, length), 0)

    def pieces(vec):
        a, b, c = split3(vec)
        a, b, c = a.astype(f32), b.astype(f32), c.astype(f32)
        return jnp.where(rows16 == 0, a, jnp.where(rows16 == 1, b, jnp.where(rows16 == 2, c, 0.0))).astype(bf16)

    for h in range(2):
        base = 64 * h
        other = 64 - base
        rows = nn(tab_ref[h], oh).astype(bf16)
        qx[h, base : base + 64, :] = qt[base : base + 64]
        qx[h, other : other + 32, :] = rows
        qx[h, other + 32 : other + 48, :] = mask.astype(bf16)
        qx[h, other + 48 : other + 64, :] = pieces(-ln_ref[h : h + 1, :])
        delta = jnp.sum(prod[base : base + 64], axis=0, keepdims=True)
        dox[h, base : base + 64, :] = dotl[base : base + 64]
        dox[h, other : other + 16, :] = pieces(-delta)
        dox[h, other + 16 : other + 64, :] = jnp.zeros((48, length), bf16)
        kt[h, 0:64, :] = ktt[base : base + 64]
        kt[h, 64:80, :] = oh
    dqt[...] = jnp.zeros_like(dqt)

    def kblock(kb, bias):
        ko = pl.multiple_of(kb * BLK, BLK)
        ks = [kx[h, pl.ds(ko, BLK), :] for h in range(2)]
        vs = [vx[h, pl.ds(ko, BLK), :] for h in range(2)]
        kts = [kt[h, :, pl.ds(ko, BLK)] for h in range(2)]

        def qblock(qb, carry):
            dk, dv = carry
            qo = pl.multiple_of(qb * BLK, BLK)
            for h in range(2):
                p = jnp.exp(nn(ks[h], qx[h, :, pl.ds(qo, BLK)]))
                dp = nn(vs[h], dox[h, :, pl.ds(qo, BLK)])
                ds = (p * dp).astype(bf16)
                dv = dv + nn(p.astype(bf16), dom[h, pl.ds(qo, BLK), :])
                dk = dk + nn(ds, qm[h, pl.ds(qo, BLK), :])
                dqt[h, :, pl.ds(qo, BLK)] += nn(kts[h], ds)
            return dk, dv

        zeros = jnp.zeros((BLK, 128), f32)
        dk, dv = lax.fori_loop(lo_ref[row, kb], hi_ref[row, kb], qblock, (zeros, zeros))
        dqkv_ref[1, pl.ds(ko, BLK), :] = dk.astype(bf16)
        dqkv_ref[2, pl.ds(ko, BLK), :] = dv.astype(bf16)
        return bias + jnp.sum(dv, axis=0, keepdims=True)

    bias_v = lax.fori_loop(0, length // BLK, kblock, jnp.zeros((1, 128), f32))
    dq = (jnp.concatenate([dqt[0, 0:64, :], dqt[1, 0:64, :]], axis=0) * 0.125).T
    dqkv_ref[0] = dq.astype(bf16)
    bias_ref[0:1, :] = jnp.sum(dq, axis=0, keepdims=True)
    bias_ref[1:2, :] = bias_v
    for h in range(2):
        by = dqt[h, 64:80, :]
        hi = by.astype(bf16)
        low = (by - hi.astype(f32)).astype(bf16)
        table_ref[h] = nt(oh, hi) + nt(oh, low)

def attend_back(qkv, segments, bands, tab, d_att, ot, ln):
    _, rows, length, width = qkv.shape
    pairs = width // 128
    lo, hi = block_ranges(segments)
    seg3 = segments.reshape(rows, 1, length)
    band3 = bands.reshape(rows, 1, length)
    part = lambda c: pl.BlockSpec((None, None, length, 128), lambda r, p, *_: (c, r, 0, p))
    rowspec = pl.BlockSpec((None, 1, length), lambda r, p, *_: (r, 0, 0))
    return pl.pallas_call(
        bwd_kernel,
        out_shape=(
            jax.ShapeDtypeStruct((3, rows, length, width), bf16),
            jax.ShapeDtypeStruct((rows, 2, width), f32),
            jax.ShapeDtypeStruct((rows, 2 * pairs, 16, 16), f32),
        ),
        grid_spec=pltpu.PrefetchScalarGridSpec(
            num_scalar_prefetch=2,
            grid=(rows, pairs),
            in_specs=[part(0), part(1), part(2), rowspec, rowspec,
                      pl.BlockSpec((2, 32, 16), lambda r, p, *_: (p, 0, 0)),
                      pl.BlockSpec((None, length, 128), lambda r, p, *_: (r, 0, p)),
                      pl.BlockSpec((None, 128, length), lambda r, p, *_: (r, p, 0)),
                      pl.BlockSpec((None, None, 2, length), lambda r, p, *_: (r, p, 0, 0))],
            out_specs=[
                pl.BlockSpec((3, None, length, 128), lambda r, p, *_: (0, r, 0, p)),
                pl.BlockSpec((None, 2, 128), lambda r, p, *_: (r, 0, p)),
                pl.BlockSpec((None, 2, 16, 16), lambda r, p, *_: (r, p, 0, 0)),
            ],
            scratch_shapes=[
                pltpu.VMEM((2, length, 128), bf16),
                pltpu.VMEM((2, 128, length), bf16),
                pltpu.VMEM((2, length, 128), bf16),
                pltpu.VMEM((2, 128, length), bf16),
                pltpu.VMEM((2, 80, length), bf16),
                pltpu.VMEM((2, length, 128), bf16),
                pltpu.VMEM((2, length, 128), bf16),
                pltpu.VMEM((2, 80, length), f32),
            ],
        ),
        name="attend_back",
    )(lo, hi, qkv, qkv, qkv, seg3, band3, tab, d_att, ot, ln)

def table_rows(band_table):
    t = jnp.swapaxes(band_table, 1, 2)
    upper = lax.reduce_precision(t, 8, 7).astype(bf16)
    lower = (t - lax.reduce_precision(t, 8, 7)).astype(bf16)
    return jnp.concatenate([upper, lower], axis=1)


norm_eps = 1e-06


def gelu_tanh(values):
    return (
        0.5
        * values
        * (1.0 + jnp.tanh(0.7978845608028654 * (values + 0.044715 * values * values * values)))
    )


def norm_forward(values, norm_gain, norm_offset):
    center = values - jnp.mean(values, axis=-1, keepdims=True)
    inv_std = lax.rsqrt(jnp.mean(center * center, axis=-1, keepdims=True) + norm_eps)
    scaled = center * inv_std
    return (scaled * norm_gain + norm_offset, scaled, inv_std)


def norm_backward(d_normed, scaled, inv_std, norm_gain):
    d_scaled = d_normed * norm_gain
    mean_grad = jnp.mean(d_scaled, axis=-1, keepdims=True)
    mean_cross = jnp.mean(d_scaled * scaled, axis=-1, keepdims=True)
    d_values = inv_std * (d_scaled - mean_grad - scaled * mean_cross)
    return (d_values, jnp.sum(d_normed * scaled, axis=0), jnp.sum(d_normed, axis=0))


def mm(a, b):
    return jnp.dot(a, b, preferred_element_type=f32)


def mm_nt(a, b):
    return lax.dot_general(a, b, (((1,), (1,)), ((), ())), preferred_element_type=f32)


def mm_tn(a, b):
    return lax.dot_general(a, b, (((0,), (0,)), ((), ())), preferred_element_type=f32)


def partner(value):
    return lax.ppermute(value, "mp", [(0, 1), (1, 0)])


def swap(value, bit, count):
    return lax.ppermute(value, "dp", [(i, i ^ bit) for i in range(count)])


def scatter_sum(value, order, count, index):
    for bit in order:
        half = value.shape[0] // 2
        side = (index // bit) % 2
        send = lax.dynamic_slice_in_dim(value, (1 - side) * half, half, 0)
        keep = lax.dynamic_slice_in_dim(value, side * half, half, 0)
        value = (keep.astype(f32) + swap(send, bit, count).astype(f32)).astype(bf16)
    return value


def gather_all(value, order, count, index):
    for bit in reversed(order):
        side = (index // bit) % 2
        got = swap(value, bit, count)
        value = jnp.where(
            side == 0, jnp.concatenate([value, got], 0), jnp.concatenate([got, value], 0)
        )
    return value


def total_sum(value, count, index):
    bits = [1 << i for i in range(count.bit_length() - 1)]
    if len(bits) < 3:
        orders = [bits]
    else:
        orders = [bits, [bits[1], bits[0]] + bits[2:], bits[2:] + bits[:2]]
    size = value.shape[0] // len(orders)
    parts = []
    for i, order in enumerate(orders):
        part = scatter_sum(value[i * size : (i + 1) * size], order, count, index)
        parts.append(gather_all(part, order, count, index).astype(f32))
    return jnp.concatenate(parts, 0)


def body(
    count,
    x_input,
    gain_attn,
    offset_attn,
    w_qkv,
    bias_qv,
    band_table,
    w_proj,
    bias_proj,
    scale_attn,
    gain_mlp,
    offset_mlp,
    w_up,
    bias_up,
    w_down,
    bias_down,
    scale_mlp,
    segments,
    bands,
    d_output,
):
    local = x_input.shape[0]
    rows_here, length = segments.shape
    tokens = rows_here * length
    width = w_qkv.shape[2]
    core = lax.axis_index("mp")
    index = lax.axis_index("dp")
    here, there = core * local, (1 - core) * local

    def join(mine, other):
        return jnp.where(
            core == 0, jnp.concatenate([mine, other], 0), jnp.concatenate([other, mine], 0)
        )

    w_up_o, w_down_o, w_proj_o, bias_up_o = (
        partner(w_up),
        partner(w_down),
        partner(w_proj),
        partner(bias_up),
    )
    valid_all = (segments.reshape(tokens) != PAGES - 1).astype(f32)[:, None]
    valid = lax.dynamic_slice_in_dim(valid_all, here, local, 0)
    x_float = x_input.astype(f32)
    normed, scaled_attn, inv_attn = norm_forward(x_float, gain_attn, offset_attn)
    normed = normed.astype(bf16)
    normed_all = join(normed, partner(normed))
    projected = jnp.einsum("td,cde->cte", normed_all, w_qkv, preferred_element_type=f32)
    bias3 = jnp.stack([bias_qv[0], jnp.zeros_like(bias_qv[0]), bias_qv[1]])[:, None, :]
    factor = jnp.array([0.125, 1.0, 1.0], bf16)[:, None, None]
    qkv = ((projected + bias3).astype(bf16) * factor).reshape(3, rows_here, length, width)
    tab = table_rows(band_table)
    attended, ot, ln = attend(qkv, segments, bands, tab)
    attended = attended.reshape(tokens, width)
    att_m = lax.dynamic_slice_in_dim(attended, here, local, 0)
    att_o = partner(lax.dynamic_slice_in_dim(attended, there, local, 0))
    attn_out = mm(att_m, w_proj) + mm(att_o, w_proj_o) + bias_proj
    hidden = x_float + scale_attn * attn_out
    normed_mlp, scaled_mlp, inv_mlp = norm_forward(hidden, gain_mlp, offset_mlp)
    normed_two = normed_mlp.astype(bf16)
    d_final = d_output.astype(f32) * valid
    d_mlp = d_final * scale_mlp
    d_mlp_low = d_mlp.astype(bf16)
    mlp_out = bias_down
    d_normed_mlp = 0.0
    grads_up, grads_down, grads_bias = [], [], []
    for up, down, bias in ((w_up_o, w_down_o, bias_up_o), (w_up, w_down, bias_up)):
        pre_act = mm(normed_two, up) + bias
        activated_full, gelu_pull = jax.vjp(gelu_tanh, pre_act)
        activated = activated_full.astype(bf16)
        mlp_out = mlp_out + mm(activated, down)
        d_pre = gelu_pull(mm_nt(d_mlp_low, down))[0]
        grads_bias.append(jnp.sum(d_pre, axis=0))
        d_pre_low = d_pre.astype(bf16)
        d_normed_mlp = d_normed_mlp + mm_nt(d_pre_low, up)
        grads_down.append(mm_tn(activated, d_mlp_low))
        grads_up.append(mm_tn(normed_two, d_pre_low))
    down_sum = (grads_down[1] + partner(grads_down[0].astype(bf16)).astype(f32)).astype(bf16)
    up_sum = (grads_up[1] + partner(grads_up[0].astype(bf16)).astype(f32)).astype(bf16)
    grad_w_down = total_sum(down_sum, count, index)
    grad_w_up = total_sum(up_sum, count, index)
    grad_bias_up = grads_bias[1] + partner(grads_bias[0])
    output = ((hidden + scale_mlp * mlp_out) * valid).astype(bf16)
    grad_scale_mlp = jnp.sum(d_final * mlp_out, axis=0)
    grad_bias_down = jnp.sum(d_mlp, axis=0)
    d_from_mlp, grad_gain_mlp, grad_offset_mlp = norm_backward(
        d_normed_mlp, scaled_mlp, inv_mlp, gain_mlp
    )
    d_hidden = d_final + d_from_mlp
    grad_scale_attn = jnp.sum(d_hidden * attn_out, axis=0)
    d_attn = d_hidden * scale_attn
    grad_bias_proj = jnp.sum(d_attn, axis=0)
    d_attn_low = d_attn.astype(bf16)
    d_att_o = partner((mm_nt(d_attn_low, w_proj_o) * valid).astype(bf16))
    d_att_m = (mm_nt(d_attn_low, w_proj) * valid).astype(bf16)
    d_att = join(d_att_m, d_att_o).reshape(rows_here, length, width)
    proj_sum = (mm_tn(att_m, d_attn_low) + partner(mm_tn(att_o, d_attn_low).astype(bf16)).astype(f32)).astype(bf16)
    grad_w_proj = total_sum(proj_sum, count, index)
    dqkv, grad_bias_rows, table_rows_grad = attend_back(qkv, segments, bands, tab, d_att, ot, ln)
    dqkv = dqkv.reshape(3, tokens, width)
    grad_bias_qv = jnp.sum(grad_bias_rows, axis=0)
    table_grad = jnp.sum(table_rows_grad, axis=0)
    d_partial = jnp.einsum("cte,cde->td", dqkv, w_qkv, preferred_element_type=f32)
    d_other = partner(lax.dynamic_slice_in_dim(d_partial, there, local, 0).astype(bf16))
    d_normed_attn = lax.dynamic_slice_in_dim(d_partial, here, local, 0) + d_other.astype(f32)
    qkv_sum = jnp.einsum("td,cte->cde", normed_all, dqkv, preferred_element_type=f32)
    grad_w_qkv = total_sum(
        qkv_sum.astype(bf16).reshape(-1, width), count, index
    ).reshape(w_qkv.shape)
    d_from_attn, grad_gain_attn, grad_offset_attn = norm_backward(
        d_normed_attn, scaled_attn, inv_attn, gain_attn
    )
    grad_input = d_hidden + d_from_attn
    shared = jnp.concatenate(
        [
            grad_gain_attn,
            grad_offset_attn,
            grad_bias_proj,
            grad_scale_attn,
            grad_gain_mlp,
            grad_offset_mlp,
            grad_bias_down,
            grad_scale_mlp,
        ]
    )
    shared = shared + partner(shared)
    own = [grad_bias_up, grad_bias_qv.reshape(-1), table_grad.reshape(-1)]
    packed = jnp.concatenate([shared] + own)
    bit = 1
    while bit < count:
        packed = packed + swap(packed, bit, count)
        bit *= 2
    wide = x_input.shape[1]
    s = [packed[i * wide : (i + 1) * wide] for i in range(8)]
    at = 8 * wide
    outs = []
    for item in own:
        outs.append(packed[at : at + item.shape[0]])
        at += item.shape[0]
    return (
        output,
        grad_input,
        s[0],
        s[1],
        grad_w_qkv,
        outs[1].reshape(bias_qv.shape),
        outs[2].reshape(band_table.shape),
        grad_w_proj,
        s[2],
        s[3],
        s[4],
        s[5],
        grad_w_up,
        outs[0],
        grad_w_down,
        s[6],
        s[7],
    )


def solution(mesh):
    tokens = P(("dp", "mp"), None)
    specs = (
        tokens, P(), P(), P(None, None, "mp"), P(None, "mp"), P("mp", None, None), P("mp", None),
        P(), P(), P(), P(), P(None, "mp"), P("mp"), P("mp", None), P(), P(), P("dp", None),
        P("dp", None), tokens,
    )
    outs = (
        tokens, tokens, P(), P(), P(None, None, "mp"), P(None, "mp"), P("mp", None, None),
        P("mp", None), P(), P(), P(), P(), P(None, "mp"), P("mp"), P("mp", None), P(), P(),
    )
    return jax.shard_map(
        functools.partial(body, mesh.shape["dp"]),
        mesh=mesh,
        in_specs=specs,
        out_specs=outs,
        check_vma=False,
    )
```

time: 1600 us -> 543 us (0.34)
  matrix products: 825 us -> 98.7 us
  waiting for transfers between devices: 366 us -> 91.9 us
  Pallas kernels: 0 us -> 148 us
  starting transfers between devices: 0.37 us -> 128 us
  other arithmetic: 166 us -> 43.9 us
  local copies, waits for them, and re-layouts: 132 us -> 27.2 us
  blocking collectives: 87.8 us -> 0 us
    dot_general x64 -> x21, matrix products: 825 us -> 98.7 us  [the longest x6 28.5 us: mm_nt(): lax.dot_general(a, b, (((1,), (1,)), ((), ())), preferred_element_type=f32)]
    psum x1 -> x0, waiting for transfers between devices: 300 us -> none  [body(): lax.psum((grad_w_up, grad_bias_up, grad_w_down, grad_w_qkv, grad_bias_qv,...]
    pallas_call x0 -> x2, Pallas kernels: none -> 148 us  [the longest x1 75.7 us: attend(): pl.pallas_call(fwd_kernel, out_shape=(jax.ShapeDtypeStruct((rows, length,...]
    ppermute x0 -> x113, starting transfers between devices: none -> 128 us  [the longest x100 125 us: swap(): return lax.ppermute(value, 'dp', [(i, i ^ bit) for i in range(count)])]
    ppermute x0 -> x113, waiting for transfers between devices: none -> 91.9 us  [the longest x100 90.4 us: swap(): return lax.ppermute(value, 'dp', [(i, i ^ bit) for i in range(count)])]
    psum x2 -> x0, blocking collectives: 87.8 us -> none  [the longest x1 84.4 us: body(): lax.psum((grad_w_up, grad_bias_up, grad_w_down, grad_w_qkv, grad_bias_qv,...]
    dynamic_update_slice x8 -> x0, local copies, waits for them, and re-layouts: 67.4 us -> none  [one_row(): lax.map(one_block, (query_row.reshape(blocks, QBLOCK, heads_here, head_si...]
    convert_element_type x19 -> x55, other arithmetic: 78.5 us -> 14.8 us  [the longest x48 9.61 us: scatter_sum(): value = (keep.astype(f32) + swap(send, bit, count).astype(f32)).astype(bf16)]
  transfers between devices with their start and end apart: 9 -> 113, of which waited for: 8 -> 48; matrix products, arithmetic and copies ran while one was open for 4% -> 21% of each run, Pallas kernels for 0% -> 13%
where the time goes in v1:
time: 543 us; the launch traced here: 541 us
  Pallas kernels  148 us (27%)
  starting transfers between devices  128 us (24%)
  matrix products  98.7 us (18%)
  waiting for transfers between devices  91.9 us (17%)
  other arithmetic  43.9 us (8%)
  local copies, waits for them, and re-layouts  27.2 us (5%)
    ppermute x100, starting transfers between devices, swap(): return lax.ppermute(value, 'dp', [(i, i ^ bit) for i in range(count)])  125 us
    ppermute x100, waiting for transfers between devices, swap(): return lax.ppermute(value, 'dp', [(i, i ^ bit) for i in range(count)])  90.4 us
    pallas_call x1, Pallas kernels, attend(): pl.pallas_call(fwd_kernel, out_shape=(jax.ShapeDtypeStruct((rows, length,...  75.7 us
    pallas_call x1, Pallas kernels, attend_back(): pl.pallas_call(bwd_kernel, out_shape=(jax.ShapeDtypeStruct((3, rows, leng...  72.3 us
    dot_general x6, matrix products, mm_nt(): lax.dot_general(a, b, (((1,), (1,)), ((), ())), preferred_element_type=f32)  28.5 us
    dot_general x6, matrix products, mm(): return jnp.dot(a, b, preferred_element_type=f32)  24.7 us
    dot_general x6, matrix products, mm_tn(): lax.dot_general(a, b, (((0,), (0,)), ((), ())), preferred_element_type=f32)  22.3 us
  transfers between devices with their start and end apart: 113, of which 48 were waited for; matrix products, arithmetic and copies ran while one was open for 21% of the time, Pallas kernels for 13%

profile of v1, /device:TPU:0, one launch (start us, length us, event | category | flops | bytes accessed | tf_op | source)
XLA Modules:
  0.0 540.7 jit_solution(7684988443133117648)
XLA Ops:
  10.3 9.5 %fusion.11.q_ref.k_ref.v_ref = bf16[3,1,2048,384]{3,2,1,0:T(8,128)(2,1)} fusion(f32[3,384]{1,0:T(4,128)S(1)} %pad_maximum_fusion.2, bf16[3,768,384]{2,1,0:T(8,128)(2,1)S(1)} %copy-done, bf16[3]{0:T(256)(128)(2,1)S(1)} %copy-done.51, bf16[1024,768]{1,0:T(8,128)(2,1)} %collective-permute-done, bf16[1024,768]{1,0:T(8,128)(2,1)} %fusion.26, pred[]{:T(512)S(6)} %eq.157), kind=kOutput, calls=%fused_computation.25 | convolution fusion | flops 3645112320 | bytes 9638407 | tf_op jit(solution)/shard_map/td,cde->cte/dot_general | solution.py:410
  19.8 75.7 %attend.1 = (bf16[1,2048,384]{2,1,0:T(8,128)(2,1)}, f32[1,384,2048]{2,1,0:T(8,128)}, f32[1,3,2,2048]{3,2,1,0:T(2,128)}) custom-call(s32[1,8]{1,0:T(1,128)} %get-tuple-element.96.lo_ref, s32[1,8]{1,0:T(1,128)} %get-tuple-element.95.hi_ref, bf16[3,1,2048,384]{3,2,1,0:T(8,128)(2,1)} %fusion.11.q_ref.k_ref.v_ref, ...), custom_call_target="tpu_custom_call" | custom-call | tf_op jit(solution)/shard_map/attend/pallas_call | solution.py:117
  106.4 3.6 multiply_convert_fusion
  110.0 7.8 %fusion.85 = (f32[1536]{0:T(1024)S(1)}, bf16[1024,1536]{1,0:T(8,128)(2,1)S(1)}) fusion(bf16[1536,768]{1,0:T(8,128)(2,1)S(1)} %copy-done.46, bf16[1024,768]{1,0:T(8,128)(2,1)S(1)} %copy-done.47, f32[1024]{0:T(1024)S(1)} %fusion.62, f32[768]{0:T(1024)S(1)} %copy-done.50, f32[1024,1536]{1,0:T(8,128)S(1)} %get-tuple-element.99, f32[1536]{0:T(1024)S(1)} %copy-done.48), kind=kOutput, calls=%fused_computation.304 | convolution fusion | flops 2459957760 | bytes 13388800 | tf_op jit(solution)/shard_map/dot_general | solution.py:314
  117.9 5.1 fusion.67
  128.2 4.3 fusion.87
  132.5 9.2 %fusion.86 = (f32[1536]{0:T(1024)S(1)}, bf16[1024,1536]{1,0:T(8,128)(2,1)S(1)}) fusion(bf16[1536,768]{1,0:T(8,128)(2,1)} %collective-permute-done.5, bf16[1024,768]{1,0:T(8,128)(2,1)S(1)} %copy-done.47, f32[1024]{0:T(1024)S(1)} %fusion.62, f32[768]{0:T(1024)S(1)} %copy-done.50, f32[1024,1536]{1,0:T(8,128)S(1)} %fusion.87, f32[1536]{0:T(1024)S(1)} %collective-permute-done.4), kind=kOutput, calls=%fused_computation.305 | convolution fusion | flops 2459957760 | bytes 13388800 | tf_op jit(solution)/shard_map/dot_general | solution.py:314
  141.7 4.0 convolution_convert_fusion.1
  145.7 5.8 %multiply_reduce_fusion.1 = (f32[768]{0:T(1024)}, f32[1024]{0:T(1024)S(1)}, f32[1024]{0:T(1024)S(1)}, f32[768]{0:T(1024)}, f32[1024,768]{1,0:T(8,128)S(1)}) fusion(f32[1024,768]{1,0:T(8,128)S(1)} %get-tuple-element.63, f32[1024]{0:T(1024)S(1)} %add_rsqrt_fusion, f32[1024]{0:T(1024)S(1)} %broadcast_multiply_fusion.4, f32[768]{0:T(1024)S(1)} %copy-done.36, ...), kind=kOutput, calls=%fused_computation.52 | convolution fusion | flops 2423779840 | bytes 14967808 | tf_op jit(solution)/shard_map/dot_general | solution.py:314
  151.5 9.3 %multiply_reduce_fusion = (f32[768]{0:T(1024)}, f32[768]{0:T(1024)}, bf16[1024,768]{1,0:T(8,128)(2,1)}, f32[768]{0:T(1024)}, f32[768]{0:T(1024)}, /*index=5*/f32[1024,768]{1,0:T(8,128)S(1)}) fusion(bf16[1024,768]{1,0:T(8,128)(2,1)S(1)} %copy-done.47, f32[1024]{0:T(1024)S(1)} %fusion.62, f32[768]{0:T(1024)S(1)} %copy-done.50, ...), kind=kOutput, calls=%fused_computation.51 | convolution fusion | flops 2450519040 | bytes 27576320 | tf_op jit(solution)/shard_map/dot_general | solution.py:310
  163.9 5.5 %convolution_convert_fusion = bf16[1536,768]{1,0:T(8,128)(2,1)} fusion(bf16[1024,768]{1,0:T(8,128)(2,1)S(1)} %copy-done.47, f32[1024]{0:T(1024)S(1)} %fusion.62, f32[768]{0:T(1024)S(1)} %copy-done.50, f32[1024,1536]{1,0:T(8,128)S(1)} %fusion.87, f32[1536]{0:T(1024)S(1)} %collective-permute-done.4), kind=kOutput, calls=%fused_computation.39 | convolution fusion | flops 2435973120 | bytes 10236928 | tf_op jit(solution)/shard_map/dot_general | solution.py:318
  180.7 6.4 %collective-permute-start.56 = (bf16[32,768]{1,0:T(8,128)(2,1)S(1)}, bf16[32,768]{1,0:T(8,128)(2,1)S(1)}, u32[]{:S(2)}, u32[]{:S(2)}) collective-permute-start(bf16[32,768]{1,0:T(8,128)(2,1)S(1)} %constant_dynamic-slice_fusion.28), channel_id=1, source_target_pairs={{0,16},{2,18},{4,20},{6,22},{8,24},{10,26},{12,28},{14,30},{16,0},... | collective-permute-start | bytes 147464 | tf_op jit(solution)/shard_map/ppermute | solution.py:326
  207.8 72.3 %attend_back.1 = (bf16[3,1,2048,384]{3,2,1,0:T(8,128)(2,1)}, f32[1,2,384]{2,1,0:T(2,128)}, f32[1,6,16,16]{3,2,1,0:T(8,128)}) custom-call(s32[1,8]{1,0:T(1,128)} %get-tuple-element.96.lo_ref, s32[1,8]{1,0:T(1,128)} %get-tuple-element.95.hi_ref, bf16[3,1,2048,384]{3,2,1,0:T(8,128)(2,1)} %fusion.11.q_ref.k_ref.v_ref, ...), custom_call_target="tpu_custom_call" | custom-call | tf_op jit(solution)/shard_map/attend_back/pallas_call | solution.py:242
  280.1 6.7 %fusion.16 = f32[2048,768]{1,0:T(8,128)S(1)} fusion(bf16[3,768,384]{2,1,0:T(8,128)(2,1)S(1)} %copy-done, bf16[3,1,2048,384]{3,2,1,0:T(8,128)(2,1)} %get-tuple-element.26), kind=kOutput, calls=%fused_computation.32 | convolution fusion | flops 3623878656 | bytes 12779520 | tf_op jit(solution)/shard_map/cte,cde->td/dot_general | solution.py:465
  290.7 7.0 %convert_bitcast_fusion = bf16[3,768,384]{1,2,0:T(8,128)(2,1)S(1)} fusion(bf16[1024,768]{1,0:T(8,128)(2,1)} %collective-permute-done, bf16[1024,768]{1,0:T(8,128)(2,1)} %fusion.26, pred[]{:T(512)S(6)} %eq.157, bf16[3,1,2048,384]{3,2,1,0:T(8,128)(2,1)S(1)} %copy-done.44), kind=kOutput, calls=%fused_computation.75 | convolution fusion | flops 3638919168 | bytes 9633793 | tf_op jit(solution)/shard_map/td,cte->cde/dot_general | solution.py:468
  316.5 5.8 %collective-permute-start.61 = (bf16[32,768]{1,0:T(8,128)(2,1)S(1)}, bf16[32,768]{1,0:T(8,128)(2,1)S(1)}, u32[]{:S(2)}, u32[]{:S(2)}) collective-permute-start(bf16[32,768]{1,0:T(8,128)(2,1)S(1)} %maximum_select_fusion.46), channel_id=1, source_target_pairs={{0,16},{2,18},{4,20},{6,22},{8,24},{10,26},{12,28},{14,30},{16,0},... | collective-permute-start | bytes 147464 | tf_op jit(solution)/shard_map/ppermute | solution.py:326
  329.0 3.5 collective-permute-done.45
  332.6 4.6 collective-permute-done.62
  337.8 4.0 collective-permute-done.54
  343.9 3.6 collective-permute-done.46
  348.9 3.4 collective-permute-start.31
  355.3 5.8 %collective-permute-done.31 = bf16[192,384]{0,1:T(8,128)(2,1)S(1)} collective-permute-done((bf16[192,384]{0,1:T(8,128)(2,1)S(1)}, bf16[192,384]{0,1:T(8,128)(2,1)S(1)}, u32[]{:S(2)}, u32[]{:S(2)}) %collective-permute-start.31) | collective-permute-done | bytes 147488 | tf_op jit(solution)/shard_map/ppermute | solution.py:326
  373.7 5.1 collective-permute-done.25
  392.9 4.5 collective-permute-done.36
  400.9 3.6 collective-permute-done.37
  408.7 5.4 %copy.45 = f32[2304,384]{1,0:T(8,128)} copy(f32[2304,384]{0,1:T(8,128)} %maximum_convert_fusion.2) | data formatting | bytes 7077888 | tf_op jit(solution)/shard_map/reshape | solution.py:471
  414.2 3.8 fusion.31
  418.3 4.4 add_convert_fusion.2
  434.0 5.9 %collective-permute-done.10 = f32[9984]{0:T(1024)S(1)} collective-permute-done((f32[9984]{0:T(1024)S(1)}, f32[9984]{0:T(1024)S(1)}, u32[]{:S(2)}, u32[]{:S(2)}) %collective-permute-start.10) | collective-permute-done | bytes 39968 | tf_op jit(solution)/shard_map/ppermute | solution.py:326
  449.6 3.5 collective-permute-done.13
  472.4 3.3 collective-permute-start.82
  512.8 3.3 collective-permute-done.94
  (537 shorter events, 231.8 us)
Async XLA Ops:
  98.2 30.0 %collective-permute-start.3 = (bf16[768,1536]{1,0:T(8,128)(2,1)}, bf16[768,1536]{1,0:T(8,128)(2,1)}, u32[]{:S(2)}, u32[]{:S(2)}) collective-permute-start(bf16[768,1536]{1,0:T(8,128)(2,1)} %param.31), channel_id=1, source_target_pairs={{0,1},{1,0},{2,3},{3,2},{4,5},{5,4},{6,7},{7,6},{8,9},{9,8},{10,11... | collective-permute-start | bytes 7077896 | tf_op jit(solution)/shard_map/ppermute | solution.py:322
  98.5 34.0 %collective-permute-start.5 = (bf16[1536,768]{1,0:T(8,128)(2,1)}, bf16[1536,768]{1,0:T(8,128)(2,1)}, u32[]{:S(2)}, u32[]{:S(2)}) collective-permute-start(bf16[1536,768]{1,0:T(8,128)(2,1)} %param.33), channel_id=1, source_target_pairs={{0,1},{1,0},{2,3},{3,2},{4,5},{5,4},{6,7},{7,6},{8,9},{9,8},{10,11... | collective-permute-start | bytes 7077896 | tf_op jit(solution)/shard_map/ppermute | solution.py:322
  98.7 33.8 %collective-permute-start.4 = (f32[1536]{0:T(1024)S(1)}, f32[1536]{0:T(1024)S(1)}, u32[]{:S(2)}, u32[]{:S(2)}) collective-permute-start(f32[1536]{0:T(1024)S(1)} %copy-done.48), channel_id=1, source_target_pairs={{0,1},{1,0},{2,3},{3,2},{4,5},{5,4},{6,7},{7,6},{8,9},{9,8},{10,11... | collective-permute-start | bytes 18440 | tf_op jit(solution)/shard_map/ppermute | solution.py:322
  163.6 10.7 %collective-permute-start.38 = (bf16[384,768]{1,0:T(8,128)(2,1)S(1)}, bf16[384,768]{1,0:T(8,128)(2,1)S(1)}, u32[]{:S(2)}, u32[]{:S(2)}) collective-permute-start(bf16[384,768]{1,0:T(8,128)(2,1)S(1)} %convolution_convert_fusion.2), channel_id=1, source_target_pairs={{0,1},{1,0},{2,3},{3,2},{4,5},{5,4},{6,7},{7,6},{8,9},{9,8},{10,11... | collective-permute-start | bytes 1769480 | tf_op jit(solution)/shard_map/ppermute | solution.py:322
  173.7 32.5 %collective-permute-start.6 = (bf16[1024,384]{1,0:T(8,128)(2,1)S(1)}, bf16[1024,384]{1,0:T(8,128)(2,1)S(1)}, u32[]{:S(2)}, u32[]{:S(2)}) collective-permute-start(bf16[1024,384]{1,0:T(8,128)(2,1)S(1)} %multiply_convert_fusion.4), channel_id=1, source_target_pairs={{0,1},{1,0},{2,3},{3,2},{4,5},{5,4},{6,7},{7,6},{8,9},{9,8},{10,11... | collective-permute-start | bytes 2359304 | tf_op jit(solution)/shard_map/ppermute | solution.py:322
  174.0 244.4 %collective-permute-start.63 = (bf16[768,1536]{1,0:T(8,128)(2,1)}, bf16[768,1536]{1,0:T(8,128)(2,1)}, u32[]{:S(2)}, u32[]{:S(2)}) collective-permute-start(bf16[768,1536]{1,0:T(8,128)(2,1)} %convolution_convert_fusion.1), channel_id=1, source_target_pairs={{0,1},{1,0},{2,3},{3,2},{4,5},{5,4},{6,7},{7,6},{8,9},{9,8},{10,11... | collective-permute-start | bytes 7077896 | tf_op jit(solution)/shard_map/ppermute | solution.py:322
  200.3 102.0 %collective-permute-start.59 = (bf16[8,768]{1,0:T(8,128)(2,1)}, bf16[8,768]{1,0:T(8,128)(2,1)}, u32[]{:S(2)}, u32[]{:S(2)}) collective-permute-start(bf16[8,768]{1,0:T(8,128)(2,1)} %add_convert_fusion.47), channel_id=1, source_target_pairs={{0,4},{2,6},{4,0},{6,2},{8,12},{10,14},{12,8},{14,10},{16,20},{18,... | collective-permute-start | bytes 36872 | tf_op jit(solution)/shard_map/ppermute | solution.py:326
  202.7 100.6 %collective-permute-start.51 = (bf16[8,768]{1,0:T(8,128)(2,1)}, bf16[8,768]{1,0:T(8,128)(2,1)}, u32[]{:S(2)}, u32[]{:S(2)}) collective-permute-start(bf16[8,768]{1,0:T(8,128)(2,1)} %add_convert_fusion.48), channel_id=1, source_target_pairs={{0,16},{2,18},{4,20},{6,22},{8,24},{10,26},{12,28},{14,30},{16,0},... | collective-permute-start | bytes 36872 | tf_op jit(solution)/shard_map/ppermute | solution.py:326
  204.3 100.4 %collective-permute-start.43 = (bf16[8,768]{1,0:T(8,128)(2,1)}, bf16[8,768]{1,0:T(8,128)(2,1)}, u32[]{:S(2)}, u32[]{:S(2)}) collective-permute-start(bf16[8,768]{1,0:T(8,128)(2,1)} %add_convert_fusion.49), channel_id=1, source_target_pairs={{0,16},{2,18},{4,20},{6,22},{8,24},{10,26},{12,28},{14,30},{16,0},... | collective-permute-start | bytes 36872 | tf_op jit(solution)/shard_map/ppermute | solution.py:326
  290.7 123.4 %collective-permute-start.7 = (bf16[1024,768]{1,0:T(8,128)(2,1)}, bf16[1024,768]{1,0:T(8,128)(2,1)}, u32[]{:S(2)}, u32[]{:S(2)}) collective-permute-start(bf16[1024,768]{1,0:T(8,128)(2,1)} %dynamic-slice_convert_fusion), channel_id=1, source_target_pairs={{0,1},{1,0},{2,3},{3,2},{4,5},{5,4},{6,7},{7,6},{8,9},{9,8},{10,11... | collective-permute-start | bytes 4718600 | tf_op jit(solution)/shard_map/ppermute | solution.py:322
  302.3 46.3 %collective-permute-start.30 = (bf16[384,384]{0,1:T(8,128)(2,1)}, bf16[384,384]{0,1:T(8,128)(2,1)S(1)}, u32[]{:S(2)}, u32[]{:S(2)}) collective-permute-start(bf16[384,384]{0,1:T(8,128)(2,1)} %dynamic-slice_bitcast_fusion.1), channel_id=1, source_target_pairs={{0,8},{2,10},{4,12},{6,14},{8,0},{10,2},{12,4},{14,6},{16,24},{18,... | collective-permute-start | bytes 884744 | tf_op jit(solution)/shard_map/ppermute | solution.py:326
  303.3 49.0 %collective-permute-start.22 = (bf16[384,384]{0,1:T(8,128)(2,1)}, bf16[384,384]{0,1:T(8,128)(2,1)S(1)}, u32[]{:S(2)}, u32[]{:S(2)}) collective-permute-start(bf16[384,384]{0,1:T(8,128)(2,1)} %dynamic-slice_bitcast_fusion.2), channel_id=1, source_target_pairs={{0,4},{2,6},{4,0},{6,2},{8,12},{10,14},{12,8},{14,10},{16,20},{18,... | collective-permute-start | bytes 884744 | tf_op jit(solution)/shard_map/ppermute | solution.py:326
  348.9 12.2 %collective-permute-start.31 = (bf16[192,384]{0,1:T(8,128)(2,1)S(1)}, bf16[192,384]{0,1:T(8,128)(2,1)S(1)}, u32[]{:S(2)}, u32[]{:S(2)}) collective-permute-start(bf16[192,384]{0,1:T(8,128)(2,1)S(1)} %constant_dynamic-slice_fusion.44), channel_id=1, source_target_pairs={{0,16},{2,18},{4,20},{6,22},{8,24},{10,26},{12,28},{14,30},{16,0},... | collective-permute-start | bytes 442376 | tf_op jit(solution)/shard_map/ppermute | solution.py:326
  368.0 10.8 %collective-permute-start.25 = (bf16[48,384]{0,1:T(8,128)(2,1)S(1)}, bf16[48,384]{0,1:T(8,128)(2,1)S(1)}, u32[]{:S(2)}, u32[]{:S(2)}) collective-permute-start(bf16[48,384]{0,1:T(8,128)(2,1)S(1)} %constant_dynamic-slice_fusion.45), channel_id=1, source_target_pairs={{0,16},{2,18},{4,20},{6,22},{8,24},{10,26},{12,28},{14,30},{16,0},... | collective-permute-start | bytes 110600 | tf_op jit(solution)/shard_map/ppermute | solution.py:326
  369.6 11.2 %collective-permute-start.17 = (bf16[48,384]{0,1:T(8,128)(2,1)S(1)}, bf16[48,384]{0,1:T(8,128)(2,1)S(1)}, u32[]{:S(2)}, u32[]{:S(2)}) collective-permute-start(bf16[48,384]{0,1:T(8,128)(2,1)S(1)} %constant_dynamic-slice_fusion.48), channel_id=1, source_target_pairs={{0,16},{2,18},{4,20},{6,22},{8,24},{10,26},{12,28},{14,30},{16,0},... | collective-permute-start | bytes 110600 | tf_op jit(solution)/shard_map/ppermute | solution.py:326
  404.5 24.4 %collective-permute-start.88 = (bf16[1536,768]{1,0:T(8,128)(2,1)}, bf16[1536,768]{1,0:T(8,128)(2,1)}, u32[]{:S(2)}, u32[]{:S(2)}) collective-permute-start(bf16[1536,768]{1,0:T(8,128)(2,1)} %convolution_convert_fusion), channel_id=1, source_target_pairs={{0,1},{1,0},{2,3},{3,2},{4,5},{5,4},{6,7},{7,6},{8,9},{9,8},{10,11... | collective-permute-start | bytes 7077896 | tf_op jit(solution)/shard_map/ppermute | solution.py:322
  418.2 13.3 %collective-permute-start.8 = (f32[6144]{0:T(1024)S(1)}, f32[6144]{0:T(1024)S(1)}, u32[]{:S(2)}, u32[]{:S(2)}) collective-permute-start(f32[6144]{0:T(1024)S(1)} %constant_dynamic-update-slice_fusion), channel_id=1, source_target_pairs={{0,1},{1,0},{2,3},{3,2},{4,5},{5,4},{6,7},{7,6},{8,9},{9,8},{10,11... | collective-permute-start | bytes 73736 | tf_op jit(solution)/shard_map/ppermute | solution.py:322
  423.8 33.1 %collective-permute-start.80 = (bf16[128,1536]{1,0:T(8,128)(2,1)}, bf16[128,1536]{1,0:T(8,128)(2,1)}, u32[]{:S(2)}, u32[]{:S(2)}) collective-permute-start(bf16[128,1536]{1,0:T(8,128)(2,1)} %constant_dynamic-slice_fusion.15), channel_id=1, source_target_pairs={{0,8},{2,10},{4,12},{6,14},{8,0},{10,2},{12,4},{14,6},{16,24},{18,... | collective-permute-start | bytes 1179656 | tf_op jit(solution)/shard_map/ppermute | solution.py:326
  426.6 32.0 %collective-permute-start.72 = (bf16[128,1536]{1,0:T(8,128)(2,1)}, bf16[128,1536]{1,0:T(8,128)(2,1)}, u32[]{:S(2)}, u32[]{:S(2)}) collective-permute-start(bf16[128,1536]{1,0:T(8,128)(2,1)} %constant_dynamic-slice_fusion.19), channel_id=1, source_target_pairs={{0,4},{2,6},{4,0},{6,2},{8,12},{10,14},{12,8},{14,10},{16,20},{18,... | collective-permute-start | bytes 1179656 | tf_op jit(solution)/shard_map/ppermute | solution.py:326
  428.0 32.5 %collective-permute-start.64 = (bf16[128,1536]{1,0:T(8,128)(2,1)}, bf16[128,1536]{1,0:T(8,128)(2,1)}, u32[]{:S(2)}, u32[]{:S(2)}) collective-permute-start(bf16[128,1536]{1,0:T(8,128)(2,1)} %constant_dynamic-slice_fusion.23), channel_id=1, source_target_pairs={{0,2},{2,0},{4,6},{6,4},{8,10},{10,8},{12,14},{14,12},{16,18},{18,... | collective-permute-start | bytes 1179656 | tf_op jit(solution)/shard_map/ppermute | solution.py:326
  434.0 29.3 %collective-permute-start.105 = (bf16[256,768]{1,0:T(8,128)(2,1)}, bf16[256,768]{1,0:T(8,128)(2,1)}, u32[]{:S(2)}, u32[]{:S(2)}) collective-permute-start(bf16[256,768]{1,0:T(8,128)(2,1)} %constant_dynamic-slice_fusion.3), channel_id=1, source_target_pairs={{0,8},{2,10},{4,12},{6,14},{8,0},{10,2},{12,4},{14,6},{16,24},{18,... | collective-permute-start | bytes 1179656 | tf_op jit(solution)/shard_map/ppermute | solution.py:326
  453.1 12.1 %collective-permute-start.97 = (bf16[256,768]{1,0:T(8,128)(2,1)}, bf16[256,768]{1,0:T(8,128)(2,1)}, u32[]{:S(2)}, u32[]{:S(2)}) collective-permute-start(bf16[256,768]{1,0:T(8,128)(2,1)} %constant_dynamic-slice_fusion.7), channel_id=1, source_target_pairs={{0,4},{2,6},{4,0},{6,2},{8,12},{10,14},{12,8},{14,10},{16,20},{18,... | collective-permute-start | bytes 1179656 | tf_op jit(solution)/shard_map/ppermute | solution.py:326
  456.9 11.8 %collective-permute-start.89 = (bf16[256,768]{1,0:T(8,128)(2,1)}, bf16[256,768]{1,0:T(8,128)(2,1)S(1)}, u32[]{:S(2)}, u32[]{:S(2)}) collective-permute-start(bf16[256,768]{1,0:T(8,128)(2,1)} %constant_dynamic-slice_fusion.11), channel_id=1, source_target_pairs={{0,2},{2,0},{4,6},{6,4},{8,10},{10,8},{12,14},{14,12},{16,18},{18,... | collective-permute-start | bytes 1179656 | tf_op jit(solution)/shard_map/ppermute | solution.py:326
  458.6 12.5 %collective-permute-start.81 = (bf16[64,1536]{1,0:T(8,128)(2,1)S(1)}, bf16[64,1536]{1,0:T(8,128)(2,1)S(1)}, u32[]{:S(2)}, u32[]{:S(2)}) collective-permute-start(bf16[64,1536]{1,0:T(8,128)(2,1)S(1)} %constant_dynamic-slice_fusion.14), channel_id=1, source_target_pairs={{0,16},{2,18},{4,20},{6,22},{8,24},{10,26},{12,28},{14,30},{16,0},... | collective-permute-start | bytes 589832 | tf_op jit(solution)/shard_map/ppermute | solution.py:326
  460.6 11.8 %collective-permute-start.73 = (bf16[64,1536]{1,0:T(8,128)(2,1)S(1)}, bf16[64,1536]{1,0:T(8,128)(2,1)S(1)}, u32[]{:S(2)}, u32[]{:S(2)}) collective-permute-start(bf16[64,1536]{1,0:T(8,128)(2,1)S(1)} %constant_dynamic-slice_fusion.18), channel_id=1, source_target_pairs={{0,2},{2,0},{4,6},{6,4},{8,10},{10,8},{12,14},{14,12},{16,18},{18,... | collective-permute-start | bytes 589832 | tf_op jit(solution)/shard_map/ppermute | solution.py:326
  463.3 12.5 %collective-permute-start.65 = (bf16[64,1536]{1,0:T(8,128)(2,1)S(1)}, bf16[64,1536]{1,0:T(8,128)(2,1)S(1)}, u32[]{:S(2)}, u32[]{:S(2)}) collective-permute-start(bf16[64,1536]{1,0:T(8,128)(2,1)S(1)} %constant_dynamic-slice_fusion.22), channel_id=1, source_target_pairs={{0,4},{2,6},{4,0},{6,2},{8,12},{10,14},{12,8},{14,10},{16,20},{18,... | collective-permute-start | bytes 589832 | tf_op jit(solution)/shard_map/ppermute | solution.py:326
  465.2 10.8 %collective-permute-start.106 = (bf16[128,768]{1,0:T(8,128)(2,1)S(1)}, bf16[128,768]{1,0:T(8,128)(2,1)S(1)}, u32[]{:S(2)}, u32[]{:S(2)}) collective-permute-start(bf16[128,768]{1,0:T(8,128)(2,1)S(1)} %constant_dynamic-slice_fusion.2), channel_id=1, source_target_pairs={{0,16},{2,18},{4,20},{6,22},{8,24},{10,26},{12,28},{14,30},{16,0},... | collective-permute-start | bytes 589832 | tf_op jit(solution)/shard_map/ppermute | solution.py:326
  505.0 11.0 %collective-permute-start.94 = (bf16[64,768]{1,0:T(8,128)(2,1)S(1)}, bf16[64,768]{1,0:T(8,128)(2,1)S(1)}, u32[]{:S(2)}, u32[]{:S(2)}) collective-permute-start(bf16[64,768]{1,0:T(8,128)(2,1)S(1)} %maximum_select_fusion.41), channel_id=1, source_target_pairs={{0,8},{2,10},{4,12},{6,14},{8,0},{10,2},{12,4},{14,6},{16,24},{18,... | collective-permute-start | bytes 294920 | tf_op jit(solution)/shard_map/ppermute | solution.py:326
  518.8 11.0 %collective-permute-start.87 = (bf16[128,1536]{1,0:T(8,128)(2,1)S(1)}, bf16[128,1536]{1,0:T(8,128)(2,1)S(1)}, u32[]{:S(2)}, u32[]{:S(2)}) collective-permute-start(bf16[128,1536]{1,0:T(8,128)(2,1)S(1)} %maximum_select_fusion.13), channel_id=1, source_target_pairs={{0,8},{2,10},{4,12},{6,14},{8,0},{10,2},{12,4},{14,6},{16,24},{18,... | collective-permute-start | bytes 1179656 | tf_op jit(solution)/shard_map/ppermute | solution.py:326
  518.9 11.8 %collective-permute-start.79 = (bf16[128,1536]{1,0:T(8,128)(2,1)S(1)}, bf16[128,1536]{1,0:T(8,128)(2,1)S(1)}, u32[]{:S(2)}, u32[]{:S(2)}) collective-permute-start(bf16[128,1536]{1,0:T(8,128)(2,1)S(1)} %maximum_select_fusion.12), channel_id=1, source_target_pairs={{0,4},{2,6},{4,0},{6,2},{8,12},{10,14},{12,8},{14,10},{16,20},{18,... | collective-permute-start | bytes 1179656 | tf_op jit(solution)/shard_map/ppermute | solution.py:326
  520.0 14.3 %collective-permute-start.71 = (bf16[128,1536]{1,0:T(8,128)(2,1)S(1)}, bf16[128,1536]{1,0:T(8,128)(2,1)S(1)}, u32[]{:S(2)}, u32[]{:S(2)}) collective-permute-start(bf16[128,1536]{1,0:T(8,128)(2,1)S(1)} %maximum_select_fusion.11), channel_id=1, source_target_pairs={{0,2},{2,0},{4,6},{6,4},{8,10},{10,8},{12,14},{14,12},{16,18},{18,... | collective-permute-start | bytes 1179656 | tf_op jit(solution)/shard_map/ppermute | solution.py:326
  521.7 12.2 %collective-permute-start.112 = (bf16[256,768]{1,0:T(8,128)(2,1)S(1)}, bf16[256,768]{1,0:T(8,128)(2,1)S(1)}, u32[]{:S(2)}, u32[]{:S(2)}) collective-permute-start(bf16[256,768]{1,0:T(8,128)(2,1)S(1)} %maximum_select_fusion.16), channel_id=1, source_target_pairs={{0,8},{2,10},{4,12},{6,14},{8,0},{10,2},{12,4},{14,6},{16,24},{18,... | collective-permute-start | bytes 1179656 | tf_op jit(solution)/shard_map/ppermute | solution.py:326
  (137 other events, 1048.6 us)
